TPU v7x, 512 devices: a whole 4x8x8 slice. The times are simulated.
512 devices in a mesh: subj: 16 (over z_lo, x, core), obj: 32 (over z_hi, y).
Axes of the slice: x: 4, y: 8, z: 8 (z_hi: 4, z_lo: 2; z = z_hi * 2 + z_lo), core: 2. Of those that a mesh axis runs over, the one named last changes fastest.
Arguments:
- subject_factors: bfloat16 [8192, 512], P(('subj', 'obj')), may hold values from -6 to 6
- object_factors: bfloat16 [16384, 512], P(('obj', 'subj')), may hold values from -6 to 6
- relations: bfloat16 [2, 512, 512], P(None, 'subj', 'obj'), may hold values from -0.01171875 to 0.01171875
- labels: int32 [2, 8192, 16384], P(None, 'subj', 'obj'), may hold values from 0 to 2
Outputs:
- grad_subject: float32 [8192, 512], P(('subj', 'obj'))
- grad_object: float32 [16384, 512], P(('obj', 'subj'))
- grad_relations: float32 [2, 512, 512], P(None, 'subj', 'obj')
- loss_rows: float32 [8192], P(('subj', 'obj'))
All inputs are finite; a program needn't handle non-finite values.
Results may differ from a plain program's by a relative error of at most 0.02.
Values may be sent and summed in bfloat16 or wider, within the bound.
No kernel may reach another device: no remote copies, remote signals or barrier semaphores. Data moves between devices by JAX's collectives and lax.ppermute only.
A program may use at most 64 MiB of HBM per device.

v0:
```python
import jax
import jax.numpy as jnp
from jax import lax
from jax.sharding import PartitionSpec as P


def sent_to_all(array, axis):
    copies = jnp.broadcast_to(array, (lax.axis_size(axis), *array.shape))
    return lax.all_to_all(copies, axis, split_axis=0, concat_axis=0, tiled=True)


def laid_out(blocks, dim):
    blocks = jnp.moveaxis(blocks, 0, dim)
    lengths = blocks.shape
    return blocks.reshape(*lengths[:dim], lengths[dim] * lengths[dim + 1], *lengths[dim + 2 :])


def collect(array, axis, dim):
    blocks = sent_to_all(array, axis)
    return laid_out(blocks, dim)


def in_blocks(array, dim, length):
    before, after = (array.shape[:dim], array.shape[dim + 1 :])
    return jnp.moveaxis(array.reshape(*before, length, -1, *after), dim, 0)


def sum_at_owner(array, axis, dim):
    length = lax.axis_size(axis)
    blocks = lax.all_to_all(in_blocks(array, dim, length), axis, 0, 0, tiled=True)
    return jnp.sum(blocks.astype(jnp.float32), axis=0)


def sent_together(arrays, axis, dim, along):
    columns = [a.reshape(*a.shape[:along], -1) for a in arrays]
    both = jnp.concatenate(columns, axis=along)
    out, at, gathered = (sum_at_owner(both, axis, dim), 0, [])
    for a, column in zip(arrays, columns):
        piece = out[..., at : at + column.shape[along]]
        gathered.append(piece.reshape(*piece.shape[:along], *a.shape[along:]))
        at += column.shape[along]
    return tuple(gathered)


def project_left(factors, relation_full):
    return jnp.einsum(
        "ic,kca->ika", factors, relation_full, preferred_element_type=jnp.float32
    ).astype(jnp.bfloat16)


def project_right(factors, relation_full):
    return jnp.einsum(
        "jc,kac->jka", factors, relation_full, preferred_element_type=jnp.float32
    ).astype(jnp.bfloat16)


def body(subject_factors, object_factors, relations, labels):
    row_pieces = collect(relations, "subj", 1)
    relation_full = collect(row_pieces, "obj", 2)
    relation_count = relation_full.shape[0]
    rank_width = relation_full.shape[1]
    subject_block = collect(subject_factors, "obj", 0)
    object_block = collect(object_factors, "subj", 0)
    left = project_left(subject_block, relation_full)
    right = project_right(object_block, relation_full)
    subject_rows = subject_block.shape[0]
    object_rows = object_block.shape[0]
    object_total = object_rows * lax.axis_size("obj")
    subject_total = subject_rows * lax.axis_size("subj")
    subject_grad = jnp.zeros((subject_rows, rank_width), jnp.float32)
    object_grad = jnp.zeros((object_rows, rank_width), jnp.float32)
    loss_sum = jnp.zeros((subject_rows,), jnp.float32)
    relation_terms = []
    for relation in range(relation_count):
        left_part = left[:, relation]
        scores = jnp.einsum(
            "ia,ja->ij", left_part, object_block, preferred_element_type=jnp.float32
        )
        codes = labels[relation]
        target = (codes == 2).astype(jnp.float32)
        weight = (codes > 0).astype(jnp.float32)
        loss_sum = loss_sum + jnp.sum(weight * (jax.nn.softplus(scores) - target * scores), axis=1)
        residual = (weight * (jax.nn.sigmoid(scores) - target)).astype(jnp.bfloat16)
        subject_grad = subject_grad + jnp.dot(
            residual, right[:, relation], preferred_element_type=jnp.float32
        )
        object_grad = object_grad + jnp.einsum(
            "ij,ia->ja", residual, left_part, preferred_element_type=jnp.float32
        )
        carried = jnp.dot(residual, object_block, preferred_element_type=jnp.float32).astype(
            jnp.bfloat16
        )
        relation_terms.append(
            jnp.einsum("ic,ia->ca", subject_block, carried, preferred_element_type=jnp.float32)
        )
    loss_part = loss_sum / (relation_count * object_total)
    grad_subject, loss_rows = sent_together(
        (subject_grad.astype(jnp.bfloat16), loss_part.astype(jnp.bfloat16)), "obj", 0, 1
    )
    grad_object = sum_at_owner(object_grad.astype(jnp.bfloat16), "subj", 0)
    relation_stack = jnp.stack(relation_terms)
    partial_rows = sum_at_owner(relation_stack.astype(jnp.bfloat16), "subj", 1)
    relation_sum = sum_at_owner(partial_rows.astype(jnp.bfloat16), "obj", 2)
    return (grad_subject, grad_object, relation_sum / subject_total, loss_rows)


def solution(mesh):
    placed = (
        P(("subj", "obj"), None),
        P(("obj", "subj"), None),
        P(None, "subj", "obj"),
        P(None, "subj", "obj"),
    )
    return jax.shard_map(
        body,
        mesh=mesh,
        in_specs=placed,
        out_specs=(
            P(("subj", "obj"), None),
            P(("obj", "subj"), None),
            P(None, "subj", "obj"),
            P(("subj", "obj")),
        ),
        check_vma=False,
    )
```

profile of v0, /device:TPU:8, one launch (start us, length us, event | category | flops | bytes accessed | tf_op | source)
XLA Modules:
  0.0 193.6 jit_solution(1295625245504654808)
XLA Ops:
  0.6 0.7 copy-done
  1.4 0.2 reshape.87
  1.5 12.1 %all_to_all.40 = bf16[16,2,512]{2,1,0:T(2,128)(2,1)S(1)} all-to-all(bf16[16,2,512]{2,1,0:T(2,128)(2,1)S(1)} %reshape.87), channel_id=1, replica_groups=mesh['subj'=16,'obj'=32] {'subj'}, dimensions={0} | all-to-all | bytes 65536 | tf_op jit(solution)/shard_map/all_to_all | solution.py:9
  13.6 1.6 broadcast_in_dim.12
  15.2 15.3 %all-to-all-start = ((bf16[32,16,512]{2,1,0:T(8,128)(2,1)}), bf16[32,16,512]{2,1,0:T(8,128)(2,1)S(1)}, u32[]{:S(2)}, u32[]{:S(2)}) async-start(bf16[32,16,512]{2,1,0:T(8,128)(2,1)} %broadcast_in_dim.12), calls=%async_computation | async-start | bytes 1048576 | tf_op jit(solution)/shard_map/all_to_all | solution.py:9
  30.5 0.1 reshape.88
  30.7 0.2 reshape.78
  30.9 20.1 %all-to-all-done = bf16[32,16,512]{2,1,0:T(8,128)(2,1)S(1)} async-done(((bf16[32,16,512]{2,1,0:T(8,128)(2,1)}), bf16[32,16,512]{2,1,0:T(8,128)(2,1)S(1)}, u32[]{:S(2)}, u32[]{:S(2)}) %all-to-all-start) | async-done | bytes 524320 | tf_op jit(solution)/shard_map/all_to_all | solution.py:9
  51.0 0.8 copy-done.4
  51.9 35.6 %all_to_all.41 = bf16[32,2,512,16]{2,3,1,0:T(8,128)(2,1)S(1)} all-to-all(bf16[32,2,512,16]{2,3,1,0:T(8,128)(2,1)S(1)} %broadcast_in_dim.14), channel_id=1, replica_groups=mesh['subj'=16,'obj'=32] {'obj'}, dimensions={0} | all-to-all | bytes 2097152 | tf_op jit(solution)/shard_map/all_to_all | solution.py:9
  87.5 0.8 broadcast_in_dim.15
  88.3 4.2 %all-to-all-start.3 = ((bf16[16,32,512]{2,1,0:T(8,128)(2,1)}), bf16[16,32,512]{2,1,0:T(8,128)(2,1)}, u32[]{:S(2)}, u32[]{:S(2)}) async-start(bf16[16,32,512]{2,1,0:T(8,128)(2,1)} %broadcast_in_dim.15), calls=%async_computation.3 | async-start | bytes 1048576 | tf_op jit(solution)/shard_map/all_to_all | solution.py:9
  92.6 1.7 fusion.12
  94.3 1.3 copy.43
  95.7 0.3 copy.42
  96.1 1.0 copy-done.2
  97.1 1.7 convolution_convert_fusion.1
  98.9 4.6 %all-to-all-done.3 = bf16[16,32,512]{2,1,0:T(8,128)(2,1)} async-done(((bf16[16,32,512]{2,1,0:T(8,128)(2,1)}), bf16[16,32,512]{2,1,0:T(8,128)(2,1)}, u32[]{:S(2)}, u32[]{:S(2)}) %all-to-all-start.3) | async-done | bytes 524320 | tf_op jit(solution)/shard_map/all_to_all | solution.py:9
  103.4 3.0 %select_convert_fusion = (bf16[512,512]{0,1:T(8,128)(2,1)S(1)}, pred[1,512,512]{1,2,0:T(8,128)(4,1)S(1)}, pred[1,512,512]{1,2,0:T(8,128)(4,1)}, f32[512,512]{0,1:T(8,128)}) fusion(s32[1,512,512]{1,2,0:T(8,128)S(1)} %copy-done.3, bf16[512,512]{1,0:T(8,128)(2,1)} %bitcast.7, bf16[512,2,512]{2,0,1:T(8,128)(2,1)} %convolution_convert_fusion.1), kind=kOutput, calls=%fused_computation.21 | convolution fusion | flops 270794752 | bytes 4194304 | tf_op jit(solution)/shard_map/ia,ja->ij/dot_general | solution.py:76
  106.4 3.1 %select_convert_fusion.1 = (bf16[512,512]{0,1:T(8,128)(2,1)S(1)}, pred[1,512,512]{1,2,0:T(8,128)(4,1)}, pred[1,512,512]{1,2,0:T(8,128)(4,1)}, f32[512,512]{0,1:T(8,128)}) fusion(s32[1,512,512]{1,2,0:T(8,128)S(1)} %copy.42, bf16[512,512]{1,0:T(8,128)(2,1)} %bitcast.7, bf16[512,2,512]{2,0,1:T(8,128)(2,1)} %convolution_convert_fusion.1), kind=kOutput, calls=%fused_computation.22 | convolution fusion | flops 270794752 | bytes 4194304 | tf_op jit(solution)/shard_map/ia,ja->ij/dot_general | solution.py:76
  109.5 1.5 fusion.9
  111.0 2.4 %fusion.1 = bf16[512,512]{1,0:T(8,128)(2,1)} fusion(f32[512,512]{1,0:T(8,128)S(1)} %fusion.9, bf16[512,512]{0,1:T(8,128)(2,1)S(1)} %get-tuple-element.4, bf16[512,2,512]{2,0,1:T(8,128)(2,1)} %convolution_convert_fusion.1), kind=kOutput, calls=%fused_computation.12 | convolution fusion | flops 268959744 | bytes 2621440 | tf_op jit(solution)/shard_map/ij,ia->ja/dot_general | solution.py:87
  113.3 3.6 %all-to-all-start.5 = ((bf16[16,32,512]{2,1,0:T(8,128)(2,1)}), bf16[16,32,512]{2,1,0:T(8,128)(2,1)S(1)}, u32[]{:S(2)}, u32[]{:S(2)}) async-start(bf16[16,32,512]{2,1,0:T(8,128)(2,1)} %bitcast.17), calls=%async_computation.5 | async-start | bytes 1048576 | tf_op jit(solution)/shard_map/all_to_all | solution.py:30
  116.9 1.9 convolution_convert_fusion.4
  118.8 1.9 convolution_convert_fusion.2
  120.7 1.1 maximum_bitcast_fusion
  121.7 6.0 %all-to-all-done.5 = bf16[16,32,512]{2,1,0:T(8,128)(2,1)S(1)} async-done(((bf16[16,32,512]{2,1,0:T(8,128)(2,1)}), bf16[16,32,512]{2,1,0:T(8,128)(2,1)S(1)}, u32[]{:S(2)}, u32[]{:S(2)}) %all-to-all-start.5) | async-done | bytes 524320 | tf_op jit(solution)/shard_map/all_to_all | solution.py:30
  127.7 3.7 %all-to-all-start.6 = ((bf16[16,2,32,512]{3,2,1,0:T(8,128)(2,1)}), bf16[16,2,32,512]{3,2,1,0:T(8,128)(2,1)S(1)}, u32[]{:S(2)}, u32[]{:S(2)}) async-start(bf16[16,2,32,512]{3,2,1,0:T(8,128)(2,1)} %maximum_bitcast_fusion), calls=%async_computation.6 | async-start | bytes 2097152 | tf_op jit(solution)/shard_map/all_to_all | solution.py:30
  131.4 2.2 %fusion.7 = f32[512]{0:T(512)S(1)} fusion(f32[512,512]{0,1:T(8,128)} %get-tuple-element.13, pred[1,512,512]{1,2,0:T(8,128)(4,1)S(1)} %copy-done.7, pred[1,512,512]{1,2,0:T(8,128)(4,1)S(1)} %get-tuple-element.5), kind=kLoop, calls=%fused_computation.18 | loop fusion | flops 2620928 | bytes 1574912 | tf_op jit(solution)/shard_map/reduce_sum | solution.py:82
  133.6 1.8 fusion.4
  135.4 0.3 convert_element_type.74
  135.6 2.1 %convolution_convert_fusion = bf16[512,2,512]{2,0,1:T(8,128)(2,1)S(1)} fusion(bf16[512,512,1]{1,0,2:T(8,128)(2,1)} %bitcast.9, bf16[2,512,512]{1,2,0:T(8,128)(2,1)} %bitcast.91), kind=kOutput, calls=%fused_computation.2 | convolution fusion | flops 537395200 | bytes 2621440 | tf_op jit(solution)/shard_map/jc,kac->jka/dot_general | solution.py:52
  137.7 0.5 fusion.8
  138.2 0.5 fusion
  138.7 0.9 pad_maximum_fusion
  139.6 8.3 %all-to-all-done.6 = bf16[16,2,32,512]{3,2,1,0:T(8,128)(2,1)S(1)} async-done(((bf16[16,2,32,512]{3,2,1,0:T(8,128)(2,1)}), bf16[16,2,32,512]{3,2,1,0:T(8,128)(2,1)S(1)}, u32[]{:S(2)}, u32[]{:S(2)}) %all-to-all-start.6) | async-done | bytes 1048608 | tf_op jit(solution)/shard_map/all_to_all | solution.py:30
  147.9 6.0 %all-to-all-start.4 = ((bf16[32,16,513]{2,1,0:T(8,128)(2,1)}), bf16[32,16,513]{2,1,0:T(8,128)(2,1)S(1)}, u32[]{:S(2)}, u32[]{:S(2)}) async-start(bf16[32,16,513]{2,1,0:T(8,128)(2,1)} %pad_maximum_fusion), calls=%async_computation.4 | async-start | bytes 1310720 | tf_op jit(solution)/shard_map/all_to_all | solution.py:30
  153.8 0.7 convert_reduce_fusion.1
  154.6 0.1 reduce_sum.61
  154.7 0.2 copy.37
  154.9 0.9 reshape.89
  155.8 20.6 %all-to-all-done.4 = bf16[32,16,513]{2,1,0:T(8,128)(2,1)S(1)} async-done(((bf16[32,16,513]{2,1,0:T(8,128)(2,1)}), bf16[32,16,513]{2,1,0:T(8,128)(2,1)S(1)}, u32[]{:S(2)}, u32[]{:S(2)}) %all-to-all-start.4) | async-done | bytes 525344 | tf_op jit(solution)/shard_map/all_to_all | solution.py:30
  176.4 4.8 %all-to-all-start.7 = ((bf16[32,2,512]{2,1,0:T(2,128)(2,1)}), bf16[32,2,512]{2,1,0:T(2,128)(2,1)S(1)}, u32[]{:S(2)}, u32[]{:S(2)}) async-start(bf16[32,2,512]{2,1,0:T(2,128)(2,1)} %reshape.89), calls=%async_computation.7 | async-start | bytes 131072 | tf_op jit(solution)/shard_map/all_to_all | solution.py:30
  181.3 0.6 slice.36
  181.9 0.6 slice_reduce_fusion
  182.6 10.1 %all-to-all-done.7 = bf16[32,2,512]{2,1,0:T(2,128)(2,1)S(1)} async-done(((bf16[32,2,512]{2,1,0:T(2,128)(2,1)}), bf16[32,2,512]{2,1,0:T(2,128)(2,1)S(1)}, u32[]{:S(2)}, u32[]{:S(2)}) %all-to-all-start.7) | async-done | bytes 65568 | tf_op jit(solution)/shard_map/all_to_all | solution.py:30
  192.7 0.2 reshape.90
  193.0 0.6 broadcast_multiply_fusion
  (26 shorter events, 0.6 us)
Async XLA Ops:
  0.6 0.7 copy-start
  15.2 35.8 %all-to-all-start = ((bf16[32,16,512]{2,1,0:T(8,128)(2,1)}), bf16[32,16,512]{2,1,0:T(8,128)(2,1)S(1)}, u32[]{:S(2)}, u32[]{:S(2)}) async-start(bf16[32,16,512]{2,1,0:T(8,128)(2,1)} %broadcast_in_dim.12), calls=%async_computation | async-start | bytes 1048576 | tf_op jit(solution)/shard_map/all_to_all | solution.py:9
  30.5 57.0 %copy-start.9 = (bf16[32,512]{1,0:T(8,128)(2,1)S(1)}, bf16[32,512]{1,0:T(8,128)(2,1)}, u32[]{:S(2)}) copy-start(bf16[32,512]{1,0:T(8,128)(2,1)} %param.5) | copy-start | bytes 98308
  50.9 0.8 copy-start.4
  88.3 15.1 %all-to-all-start.3 = ((bf16[16,32,512]{2,1,0:T(8,128)(2,1)}), bf16[16,32,512]{2,1,0:T(8,128)(2,1)}, u32[]{:S(2)}, u32[]{:S(2)}) async-start(bf16[16,32,512]{2,1,0:T(8,128)(2,1)} %broadcast_in_dim.15), calls=%async_computation.3 | async-start | bytes 1048576 | tf_op jit(solution)/shard_map/all_to_all | solution.py:9
  96.0 1.1 copy-start.5
  96.0 7.4 %copy-start.3 = (s32[1,512,512]{1,2,0:T(8,128)S(1)}, s32[1,512,512]{1,2,0:T(8,128)}, u32[]{:S(2)}) copy-start(s32[1,512,512]{1,2,0:T(8,128)} %copy.43) | copy-start | bytes 3145732
  96.1 1.0 copy-start.2
  111.0 5.9 %copy-start.6 = (bf16[32,16,512]{2,1,0:T(8,128)(2,1)S(1)}, bf16[32,16,512]{2,1,0:T(8,128)(2,1)}, u32[]{:S(2)}) copy-start(bf16[32,16,512]{2,1,0:T(8,128)(2,1)} %copy-done.4) | copy-start | bytes 1572868
  113.3 14.4 %all-to-all-start.5 = ((bf16[16,32,512]{2,1,0:T(8,128)(2,1)}), bf16[16,32,512]{2,1,0:T(8,128)(2,1)S(1)}, u32[]{:S(2)}, u32[]{:S(2)}) async-start(bf16[16,32,512]{2,1,0:T(8,128)(2,1)} %bitcast.17), calls=%async_computation.5 | async-start | bytes 1048576 | tf_op jit(solution)/shard_map/all_to_all | solution.py:30
  121.7 9.7 %copy-start.7 = (pred[1,512,512]{1,2,0:T(8,128)(4,1)S(1)}, pred[1,512,512]{1,2,0:T(8,128)(4,1)}, u32[]{:S(2)}) copy-start(pred[1,512,512]{1,2,0:T(8,128)(4,1)} %get-tuple-element.6) | copy-start | bytes 786436
  121.7 11.8 %copy-start.8 = (pred[1,512,512]{1,2,0:T(8,128)(4,1)S(1)}, pred[1,512,512]{1,2,0:T(8,128)(4,1)}, u32[]{:S(2)}) copy-start(pred[1,512,512]{1,2,0:T(8,128)(4,1)} %get-tuple-element.8) | copy-start | bytes 786436
  127.7 20.2 %all-to-all-start.6 = ((bf16[16,2,32,512]{3,2,1,0:T(8,128)(2,1)}), bf16[16,2,32,512]{3,2,1,0:T(8,128)(2,1)S(1)}, u32[]{:S(2)}, u32[]{:S(2)}) async-start(bf16[16,2,32,512]{3,2,1,0:T(8,128)(2,1)} %maximum_bitcast_fusion), calls=%async_computation.6 | async-start | bytes 2097152 | tf_op jit(solution)/shard_map/all_to_all | solution.py:30
  131.4 2.2 %copy-start.1 = (f32[512,512]{0,1:T(8,128)S(1)}, f32[512,512]{0,1:T(8,128)}, u32[]{:S(2)}) copy-start(f32[512,512]{0,1:T(8,128)} %get-tuple-element.12) | copy-start | bytes 3145732
  147.9 28.5 %all-to-all-start.4 = ((bf16[32,16,513]{2,1,0:T(8,128)(2,1)}), bf16[32,16,513]{2,1,0:T(8,128)(2,1)S(1)}, u32[]{:S(2)}, u32[]{:S(2)}) async-start(bf16[32,16,513]{2,1,0:T(8,128)(2,1)} %pad_maximum_fusion), calls=%async_computation.4 | async-start | bytes 1310720 | tf_op jit(solution)/shard_map/all_to_all | solution.py:30
  176.4 16.3 %all-to-all-start.7 = ((bf16[32,2,512]{2,1,0:T(2,128)(2,1)}), bf16[32,2,512]{2,1,0:T(2,128)(2,1)S(1)}, u32[]{:S(2)}, u32[]{:S(2)}) async-start(bf16[32,2,512]{2,1,0:T(2,128)(2,1)} %reshape.89), calls=%async_computation.7 | async-start | bytes 131072 | tf_op jit(solution)/shard_map/all_to_all | solution.py:30
where the time goes:
time: 195 us; the launch traced here: 194 us
  waiting for transfers between devices  69.7 us (36%)
  blocking collectives  47.7 us (24%)
  starting transfers between devices  37.5 us (19%)
  matrix products  18.4 us (9%)
  local copies, waits for them, and re-layouts  11.8 us (6%)
  other arithmetic  7.58 us (4%)
    all_to_all x2, blocking collectives, sent_to_all(): return lax.all_to_all(copies, axis, split_axis=0, concat_axis=0, tiled=True)  47.7 us
    all_to_all x4, waiting for transfers between devices, sum_at_owner(): lax.all_to_all(in_blocks(array, dim, length), axis, 0, 0, tiled=True)  45 us
    all_to_all x2, waiting for transfers between devices, sent_to_all(): return lax.all_to_all(copies, axis, split_axis=0, concat_axis=0, tiled=True)  24.7 us
    all_to_all x2, starting transfers between devices, sent_to_all(): return lax.all_to_all(copies, axis, split_axis=0, concat_axis=0, tiled=True)  19.5 us
    all_to_all x4, starting transfers between devices, sum_at_owner(): lax.all_to_all(in_blocks(array, dim, length), axis, 0, 0, tiled=True)  18 us
    dot_general x2, matrix products, body(): jnp.einsum('ia,ja->ij', left_part, object_block, preferred_element_type=j...  6.08 us
    unnamed x27, local copies, waits for them, and re-layouts  5.58 us
    reduce_sum x2, other arithmetic, body(): jnp.sum(weight * (jax.nn.softplus(scores) - target * scores), axis=1)  3.94 us
  transfers between devices with their start and end apart: 6, of which 6 were waited for; matrix products, arithmetic and copies ran while one was open for 11% of the time, Pallas kernels for 0%

commit v1 on v0

v1 whole, which is shorter than its diff:
```python
import jax
import jax.numpy as jnp
from jax import lax
from jax.experimental import pallas as pl
from jax.experimental.pallas import tpu as pltpu
from jax.sharding import PartitionSpec as P

F32 = jnp.float32
BF16 = jnp.bfloat16
LANES = 128
CHUNK = 128


def halves_to_lanes(rows):
    return jnp.concatenate([rows[:, :8], rows[:, 8:]], axis=2)


def lanes_to_halves(tile):
    half = tile.shape[2] // 2
    return jnp.concatenate([tile[:, :, :half], tile[:, :, half:]], axis=1)


def columns_to_rows(block):
    return jnp.concatenate(
        [block[:, c : c + LANES] for c in range(0, block.shape[1], LANES)], axis=0
    )


def dot(a, b, contract):
    return lax.dot_general(a, b, ((contract[:1], contract[1:]), ((), ())), preferred_element_type=F32)


def pack_subject(subject_ref, relation_ref, out_ref):
    copies, _, _ = out_ref.shape
    turned = jnp.concatenate([relation_ref[0], relation_ref[1]], axis=1).astype(F32)
    tile = halves_to_lanes(turned[None])[0].astype(BF16)
    factors = columns_to_rows(subject_ref[...])
    split = factors.shape[0]
    for p in range(copies):
        out_ref[p, :split] = factors
        out_ref[p, split:] = tile


def pack_object(gathered_ref, object_ref, out_ref):
    copies, _, width = out_ref.shape
    rows = object_ref.shape[0]
    split = gathered_ref.shape[1] - 8
    tiles = gathered_ref[:, split:, :].astype(F32)
    turned = lanes_to_halves(tiles)
    rel = turned.reshape(width, turned.shape[2]).T.astype(BF16)
    own = object_ref[...]
    for p in range(copies):
        out_ref[p, :rows] = own
        out_ref[p, rows:] = rel


def object_rows(gathered_ref, rows):
    part = gathered_ref[:, :rows, :]
    return part.reshape(-1, part.shape[2])


def relation_rows(gathered_ref, relation, rows):
    start = rows * (relation + 1)
    part = gathered_ref[:, start : start + rows, :]
    return part.reshape(-1, part.shape[2])


def grads(subject_ref, object_ref, labels_ref, out_ref, left_ref, carried_ref, residual_ref):
    relations, size, _ = labels_ref.shape
    rows = size // out_ref.shape[0]
    owners = subject_ref.shape[0]
    per_owner = size // owners
    subject = jnp.concatenate(
        [
            subject_ref[:, c * per_owner : (c + 1) * per_owner, :].reshape(size, LANES)
            for c in range(size // LANES)
        ],
        axis=1,
    )
    objects = object_rows(object_ref, rows)
    for k in range(relations):
        rel = relation_rows(object_ref, k, rows)
        left_ref[k] = dot(subject, rel, (1, 0)).astype(BF16)
        for at in range(0, size, CHUNK):
            span = pl.ds(at, CHUNK)
            scores = dot(left_ref[k, span], objects, (1, 1))
            codes = labels_ref[k, span]
            small = jnp.exp(-jnp.abs(scores))
            scale = 1.0 / (1.0 + small)
            sigmoid = jnp.where(scores >= 0.0, scale, small * scale)
            target = jnp.where(codes == 2, 1.0, 0.0)
            residual = jnp.where(codes > 0, sigmoid - target, 0.0).astype(BF16)
            residual_ref[k, span] = residual
            carried_ref[k, span] = dot(residual, objects, (1, 0)).astype(BF16)
        grad = dot(subject, carried_ref[k], (0, 0)).astype(BF16)
        out_ref[:, rows * (k + 1) : rows * (k + 2), :] = grad.reshape(-1, rows, size)
    grad_object = dot(residual_ref[0], left_ref[0], (0, 0))
    for k in range(1, relations):
        grad_object = grad_object + dot(residual_ref[k], left_ref[k], (0, 0))
    out_ref[:, :rows, :] = grad_object.astype(BF16).reshape(-1, rows, size)


def subject_grads(object_ref, labels_ref, left_ref, carried_ref, out_ref, *, total):
    relations, size, _ = labels_ref.shape
    rows = size // object_ref.shape[0]
    owners = out_ref.shape[0]
    per_owner = size // owners
    objects = object_rows(object_ref, rows)
    here = CHUNK // per_owner
    for at in range(0, size, CHUNK):
        span = pl.ds(at, CHUNK)
        loss = jnp.zeros((CHUNK, 1), F32)
        grad = jnp.zeros((CHUNK, size), F32)
        for k in range(relations):
            scores = dot(left_ref[k, span], objects, (1, 1))
            codes = labels_ref[k, span]
            soft = jnp.maximum(scores, 0.0) + jnp.log1p(jnp.exp(-jnp.abs(scores)))
            cell = jnp.where(codes == 2, soft - scores, soft)
            loss = loss + jnp.sum(jnp.where(codes > 0, cell, 0.0), axis=1, keepdims=True)
            grad = grad + dot(carried_ref[k, span], relation_rows(object_ref, k, rows), (1, 1))
        first = at // per_owner
        grad = grad.astype(BF16).reshape(here, per_owner, size)
        for c in range(size // LANES):
            out_ref[first : first + here, c * per_owner : (c + 1) * per_owner, :] = grad[
                :, :, c * LANES : (c + 1) * LANES
            ]
        part = jnp.broadcast_to(loss / total, (CHUNK, LANES // 2)).reshape(here, per_owner, -1)
        split = size // LANES * per_owner
        out_ref[first : first + here, split : split + 8, :] = halves_to_lanes(part).astype(BF16)


def sum_object(partial_ref, subject_ref, grad_ref, out_ref):
    rows = grad_ref.shape[0]
    width = grad_ref.shape[1]
    total = jnp.sum(partial_ref[...].astype(F32), axis=0)
    grad_ref[...] = total[:rows]
    turned = total[rows:].T
    owners = subject_ref.shape[0]
    tiles = halves_to_lanes(turned.reshape(owners, width // owners, -1)).astype(BF16)
    split = subject_ref.shape[1]
    out_ref[:, :split, :] = subject_ref[...]
    out_ref[:, split:, :] = tiles


def sum_subject(partial_ref, grad_ref, relation_ref, loss_ref, *, total):
    rows, width = grad_ref.shape
    summed = jnp.sum(partial_ref[...].astype(F32), axis=0)
    blocks = width // LANES
    grad_ref[...] = jnp.concatenate(
        [summed[c * rows : (c + 1) * rows] for c in range(blocks)], axis=1
    )
    at = blocks * rows
    loss = lanes_to_halves(summed[None, at : at + 8])[0]
    loss_ref[...] = loss.T[:1]
    turned = lanes_to_halves(summed[None, at + 8 : at + 16])[0] * (1.0 / total)
    columns = relation_ref.shape[2]
    for k in range(relation_ref.shape[0]):
        relation_ref[k] = turned[:, k * columns : (k + 1) * columns]


def shape(dims, dtype=BF16):
    return jax.ShapeDtypeStruct(dims, dtype)


def call(kernel, name, outs, *args, scratch=()):
    return pl.pallas_call(kernel, out_shape=outs, scratch_shapes=scratch, name=name)(*args)


def body(subject_factors, object_factors, relations, labels):
    subj, obj = lax.axis_size("subj"), lax.axis_size("obj")
    subject_rows, width = subject_factors.shape
    object_part = object_factors.shape[0]
    count, rel_rows, rel_columns = relations.shape
    _, subjects, objects = labels.shape
    strips = width // LANES * subject_rows
    turned = jnp.swapaxes(relations, 1, 2)
    sent = call(pack_subject, "pack_subject", shape((obj, strips + 8, LANES)), subject_factors, turned)
    subject_all = lax.all_to_all(sent, "obj", 0, 0, tiled=True)
    stacked = object_part + count * rel_rows
    sent = call(
        pack_object, "pack_object", shape((subj, stacked, width)), subject_all, object_factors
    )
    object_all = lax.all_to_all(sent, "subj", 0, 0, tiled=True)
    square = (count, subjects, width)
    partial, left, carried = call(
        grads,
        "grads",
        (shape((subj, stacked, width)), shape(square), shape(square)),
        subject_all,
        object_all,
        labels,
        scratch=[pltpu.VMEM((count, subjects, objects), BF16)],
    )
    received = lax.all_to_all(partial, "subj", 0, 0, tiled=True)
    scale = float(count * objects * obj)
    packed = call(
        lambda *refs: subject_grads(*refs, total=scale),
        "subject_grads",
        shape((obj, strips + 8, LANES)),
        object_all,
        labels,
        left,
        carried,
    )
    grad_object, sent = call(
        sum_object,
        "sum_object",
        (shape((object_part, width), F32), shape((obj, strips + 16, LANES))),
        received,
        packed,
    )
    received = lax.all_to_all(sent, "obj", 0, 0, tiled=True)
    scale = float(subjects * subj)
    grad_subject, grad_relations, loss = call(
        lambda *refs: sum_subject(*refs, total=scale),
        "sum_subject",
        (
            shape((subject_rows, width), F32),
            shape((count, rel_columns, rel_rows), F32),
            shape((1, subject_rows), F32),
        ),
        received,
    )
    return grad_subject, grad_object, jnp.swapaxes(grad_relations, 1, 2), loss.reshape(subject_rows)


def solution(mesh):
    placed = (
        P(("subj", "obj"), None),
        P(("obj", "subj"), None),
        P(None, "subj", "obj"),
        P(None, "subj", "obj"),
    )
    return jax.shard_map(
        body,
        mesh=mesh,
        in_specs=placed,
        out_specs=(
            P(("subj", "obj"), None),
            P(("obj", "subj"), None),
            P(None, "subj", "obj"),
            P(("subj", "obj")),
        ),
        check_vma=False,
    )
```

time: 195 us -> 138 us (0.71)
  the two profiles are of different devices: /device:TPU:8 before, /device:TPU:14 now
where the time goes in v1:
time: 138 us
  blocking collectives  91.5 us (66%)
  Pallas kernels  23.8 us (17%)
  waiting for transfers between devices  14.8 us (11%)
  starting transfers between devices  5.86 us (4%)
    all_to_all x1, blocking collectives, body(): subject_all = lax.all_to_all(sent, 'obj', 0, 0, tiled=True)  37.8 us
    all_to_all x1, blocking collectives, body(): received = lax.all_to_all(sent, 'obj', 0, 0, tiled=True)  28.1 us
    all_to_all x1, blocking collectives, body(): object_all = lax.all_to_all(sent, 'subj', 0, 0, tiled=True)  25.6 us
    pallas_call x6, Pallas kernels, call(): pl.pallas_call(kernel, out_shape=outs, scratch_shapes=scratch, name=name)  23.8 us
    all_to_all x1, waiting for transfers between devices, body(): received = lax.all_to_all(partial, 'subj', 0, 0, tiled=True)  14.8 us
    all_to_all x1, starting transfers between devices, body(): received = lax.all_to_all(partial, 'subj', 0, 0, tiled=True)  5.86 us
  transfers between devices with their start and end apart: 1, of which 1 were waited for; matrix products, arithmetic and copies ran while one was open for 0% of the time, Pallas kernels for 5%

profile of v1, /device:TPU:14, one launch (start us, length us, event | category | flops | bytes accessed | tf_op | source)
XLA Modules:
  0.0 137.8 jit_solution(2131867475428445576)
XLA Ops:
  0.6 1.7 %pack_subject.1 = bf16[32,72,128]{2,1,0:T(8,128)(2,1)} custom-call(bf16[16,512]{1,0:T(8,128)(2,1)} %subject_ref.1, bf16[2,16,32]{2,1,0:T(8,128)(2,1)} %bitcast.3), custom_call_target="tpu_custom_call" | custom-call | tf_op jit(solution)/shard_map/pack_subject/pallas_call | solution.py:166
  2.3 37.8 %all_to_all.20.gathered_ref.subject_ref = bf16[32,72,128]{2,1,0:T(8,128)(2,1)} all-to-all(bf16[32,72,128]{2,1,0:T(8,128)(2,1)} %pack_subject.1), channel_id=1, replica_groups=mesh['subj'=16,'obj'=32] {'obj'}, dimensions={0} | all-to-all | bytes 1179648 | tf_op jit(solution)/shard_map/all_to_all | solution.py:178
  40.1 2.5 %pack_object.1 = bf16[16,96,512]{2,1,0:T(8,128)(2,1)} custom-call(bf16[32,72,128]{2,1,0:T(8,128)(2,1)} %all_to_all.20.gathered_ref.subject_ref, bf16[32,512]{1,0:T(8,128)(2,1)} %object_ref.1), custom_call_target="tpu_custom_call" | custom-call | tf_op jit(solution)/shard_map/pack_object/pallas_call | solution.py:166
  42.6 25.6 %all_to_all.21.object_ref.refs_0_ = bf16[16,96,512]{2,1,0:T(8,128)(2,1)} all-to-all(bf16[16,96,512]{2,1,0:T(8,128)(2,1)} %pack_object.1), channel_id=1, replica_groups=mesh['subj'=16,'obj'=32] {'subj'}, dimensions={0} | all-to-all | bytes 3145728 | tf_op jit(solution)/shard_map/all_to_all | solution.py:183
  68.2 8.4 %grads.1 = (bf16[16,96,512]{2,1,0:T(8,128)(2,1)}, bf16[2,512,512]{2,1,0:T(8,128)(2,1)}, bf16[2,512,512]{2,1,0:T(8,128)(2,1)}) custom-call(bf16[32,72,128]{2,1,0:T(8,128)(2,1)} %all_to_all.20.gathered_ref.subject_ref, bf16[16,96,512]{2,1,0:T(8,128)(2,1)} %all_to_all.21.object_ref.refs_0_, s32[2,512,512]{2,1,0:T(8,128)} %refs_1_.1), custom_call_target="tpu_custom_call" | custom-call | tf_op jit(solution)/shard_map/grads/pallas_call | solution.py:166
  76.5 5.9 %all-to-all-start.2 = ((bf16[16,96,512]{2,1,0:T(8,128)(2,1)}), bf16[16,96,512]{2,1,0:T(8,128)(2,1)S(1)}, u32[]{:S(2)}, u32[]{:S(2)}) async-start(bf16[16,96,512]{2,1,0:T(8,128)(2,1)} %get-tuple-element.12), calls=%async_computation.2 | async-start | bytes 3145728 | tf_op jit(solution)/shard_map/all_to_all | solution.py:194
  82.4 6.7 %subject_grads.1.subject_ref = bf16[32,72,128]{2,1,0:T(8,128)(2,1)} custom-call(bf16[16,96,512]{2,1,0:T(8,128)(2,1)} %all_to_all.21.object_ref.refs_0_, s32[2,512,512]{2,1,0:T(8,128)} %refs_1_.1, bf16[2,512,512]{2,1,0:T(8,128)(2,1)} %get-tuple-element.13.refs_2_, bf16[2,512,512]{2,1,0:T(8,128)(2,1)} %get-tuple-element.14.refs_3_), custom_call_target="tpu_custom_call" | custom-call | tf_op jit(solution)/shard_map/subject_grads/pallas_call | solution.py:166
  89.1 14.8 %all-to-all-done.2.partial_ref = bf16[16,96,512]{2,1,0:T(8,128)(2,1)S(1)} async-done(((bf16[16,96,512]{2,1,0:T(8,128)(2,1)}), bf16[16,96,512]{2,1,0:T(8,128)(2,1)S(1)}, u32[]{:S(2)}, u32[]{:S(2)}) %all-to-all-start.2) | async-done | bytes 1572896 | tf_op jit(solution)/shard_map/all_to_all | solution.py:194
  103.9 0.0 copy-start
  103.9 1.2 copy-done
  105.1 2.7 %sum_object.1 = (f32[32,512]{1,0:T(8,128)}, bf16[32,80,128]{2,1,0:T(8,128)(2,1)}) custom-call(bf16[16,96,512]{2,1,0:T(8,128)(2,1)} %copy-done, bf16[32,72,128]{2,1,0:T(8,128)(2,1)} %subject_grads.1.subject_ref), custom_call_target="tpu_custom_call" | custom-call | tf_op jit(solution)/shard_map/sum_object/pallas_call | solution.py:166
  107.8 28.1 %all_to_all.22.refs_0_ = bf16[32,80,128]{2,1,0:T(8,128)(2,1)} all-to-all(bf16[32,80,128]{2,1,0:T(8,128)(2,1)} %get-tuple-element.15), channel_id=1, replica_groups=mesh['subj'=16,'obj'=32] {'obj'}, dimensions={0} | all-to-all | bytes 1310720 | tf_op jit(solution)/shard_map/all_to_all | solution.py:212
  135.9 1.9 %sum_subject.1 = (f32[16,512]{1,0:T(8,128)}, f32[2,16,32]{2,1,0:T(8,128)}, f32[1,16]{1,0:T(1,128)}) custom-call(bf16[32,80,128]{2,1,0:T(8,128)(2,1)} %all_to_all.22.refs_0_), custom_call_target="tpu_custom_call" | custom-call | tf_op jit(solution)/shard_map/sum_subject/pallas_call | solution.py:166
Async XLA Ops:
  76.5 27.4 %all-to-all-start.2 = ((bf16[16,96,512]{2,1,0:T(8,128)(2,1)}), bf16[16,96,512]{2,1,0:T(8,128)(2,1)S(1)}, u32[]{:S(2)}, u32[]{:S(2)}) async-start(bf16[16,96,512]{2,1,0:T(8,128)(2,1)} %get-tuple-element.12), calls=%async_computation.2 | async-start | bytes 3145728 | tf_op jit(solution)/shard_map/all_to_all | solution.py:194
  103.9 1.2 copy-start

commit v2 on v1

--- a/solution.py
+++ b/solution.py
@@ -3,6 +3,7 @@
 from jax import lax
 from jax.experimental import pallas as pl
 from jax.experimental.pallas import tpu as pltpu
+from jax.sharding import Mesh
 from jax.sharding import PartitionSpec as P
 
 F32 = jnp.float32
@@ -54,20 +55,37 @@
         out_ref[p, rows:] = rel
 
 
-def object_rows(gathered_ref, rows):
-    part = gathered_ref[:, :rows, :]
-    return part.reshape(-1, part.shape[2])
-
-
-def relation_rows(gathered_ref, relation, rows):
-    start = rows * (relation + 1)
-    part = gathered_ref[:, start : start + rows, :]
-    return part.reshape(-1, part.shape[2])
-
-
-def grads(subject_ref, object_ref, labels_ref, out_ref, left_ref, carried_ref, residual_ref):
+def stacked_rows(own_ref, other_ref, part, rows):
+    first = lax.axis_index("core") == 0
+    own = own_ref[:, rows * part : rows * (part + 1), :]
+    other = other_ref[:, rows * part : rows * (part + 1), :]
+    even = jnp.where(first, own, other)
+    odd = jnp.where(first, other, own)
+    return jnp.stack([even, odd], axis=1).reshape(-1, own.shape[2])
+
+
+def store_owners(keep_ref, send_ref, part, rows, values):
+    first = lax.axis_index("core") == 0
+    by_core = values.reshape(keep_ref.shape[0], 2, rows, values.shape[1])
+    even, odd = by_core[:, 0], by_core[:, 1]
+    span = slice(rows * part, rows * (part + 1))
+    keep_ref[:, span, :] = jnp.where(first, even, odd).astype(BF16)
+    send_ref[:, span, :] = jnp.where(first, odd, even).astype(BF16)
+
+
+def grads(
+    subject_ref,
+    own_ref,
+    other_ref,
+    labels_ref,
+    keep_ref,
+    send_ref,
+    left_ref,
+    carried_ref,
+    residual_ref,
+):
     relations, size, _ = labels_ref.shape
-    rows = size // out_ref.shape[0]
+    rows = size // (2 * keep_ref.shape[0])
     owners = subject_ref.shape[0]
     per_owner = size // owners
     subject = jnp.concatenate(
@@ -77,9 +95,9 @@
         ],
         axis=1,
     )
-    objects = object_rows(object_ref, rows)
+    objects = stacked_rows(own_ref, other_ref, 0, rows)
     for k in range(relations):
-        rel = relation_rows(object_ref, k, rows)
+        rel = stacked_rows(own_ref, other_ref, k + 1, rows)
         left_ref[k] = dot(subject, rel, (1, 0)).astype(BF16)
         for at in range(0, size, CHUNK):
             span = pl.ds(at, CHUNK)
@@ -92,20 +110,24 @@
             residual = jnp.where(codes > 0, sigmoid - target, 0.0).astype(BF16)
             residual_ref[k, span] = residual
             carried_ref[k, span] = dot(residual, objects, (1, 0)).astype(BF16)
-        grad = dot(subject, carried_ref[k], (0, 0)).astype(BF16)
-        out_ref[:, rows * (k + 1) : rows * (k + 2), :] = grad.reshape(-1, rows, size)
+        store_owners(keep_ref, send_ref, k + 1, rows, dot(subject, carried_ref[k], (0, 0)))
     grad_object = dot(residual_ref[0], left_ref[0], (0, 0))
     for k in range(1, relations):
         grad_object = grad_object + dot(residual_ref[k], left_ref[k], (0, 0))
-    out_ref[:, :rows, :] = grad_object.astype(BF16).reshape(-1, rows, size)
-
-
-def subject_grads(object_ref, labels_ref, left_ref, carried_ref, out_ref, *, total):
+    store_owners(keep_ref, send_ref, 0, rows, grad_object)
+
+
+def add_pair(keep_ref, received_ref, out_ref):
+    out_ref[...] = (keep_ref[...].astype(F32) + received_ref[...].astype(F32)).astype(BF16)
+
+
+def subject_grads(own_ref, other_ref, labels_ref, left_ref, carried_ref, out_ref, *, total):
     relations, size, _ = labels_ref.shape
-    rows = size // object_ref.shape[0]
+    rows = size // (2 * own_ref.shape[0])
     owners = out_ref.shape[0]
     per_owner = size // owners
-    objects = object_rows(object_ref, rows)
+    objects = stacked_rows(own_ref, other_ref, 0, rows)
+    rels = [stacked_rows(own_ref, other_ref, k + 1, rows) for k in range(relations)]
     here = CHUNK // per_owner
     for at in range(0, size, CHUNK):
         span = pl.ds(at, CHUNK)
@@ -117,7 +139,7 @@
             soft = jnp.maximum(scores, 0.0) + jnp.log1p(jnp.exp(-jnp.abs(scores)))
             cell = jnp.where(codes == 2, soft - scores, soft)
             loss = loss + jnp.sum(jnp.where(codes > 0, cell, 0.0), axis=1, keepdims=True)
-            grad = grad + dot(carried_ref[k, span], relation_rows(object_ref, k, rows), (1, 1))
+            grad = grad + dot(carried_ref[k, span], rels[k], (1, 1))
         first = at // per_owner
         grad = grad.astype(BF16).reshape(here, per_owner, size)
         for c in range(size // LANES):
@@ -166,8 +188,13 @@
     return pl.pallas_call(kernel, out_shape=outs, scratch_shapes=scratch, name=name)(*args)
 
 
+def to_other_core(array):
+    return lax.ppermute(array, "core", [(0, 1), (1, 0)])
+
+
 def body(subject_factors, object_factors, relations, labels):
-    subj, obj = lax.axis_size("subj"), lax.axis_size("obj")
+    chips, obj = lax.axis_size("chip"), lax.axis_size("obj")
+    subj = 2 * chips
     subject_rows, width = subject_factors.shape
     object_part = object_factors.shape[0]
     count, rel_rows, rel_columns = relations.shape
@@ -176,28 +203,30 @@
     turned = jnp.swapaxes(relations, 1, 2)
     sent = call(pack_subject, "pack_subject", shape((obj, strips + 8, LANES)), subject_factors, turned)
     subject_all = lax.all_to_all(sent, "obj", 0, 0, tiled=True)
-    stacked = object_part + count * rel_rows
-    sent = call(
-        pack_object, "pack_object", shape((subj, stacked, width)), subject_all, object_factors
-    )
-    object_all = lax.all_to_all(sent, "subj", 0, 0, tiled=True)
+    stacked = (chips, object_part + count * rel_rows, width)
+    sent = call(pack_object, "pack_object", shape(stacked), subject_all, object_factors)
+    own = lax.all_to_all(sent, "chip", 0, 0, tiled=True)
+    other = to_other_core(own)
     square = (count, subjects, width)
-    partial, left, carried = call(
+    keep, send, left, carried = call(
         grads,
         "grads",
-        (shape((subj, stacked, width)), shape(square), shape(square)),
+        (shape(stacked), shape(stacked), shape(square), shape(square)),
         subject_all,
-        object_all,
+        own,
+        other,
         labels,
         scratch=[pltpu.VMEM((count, subjects, objects), BF16)],
     )
-    received = lax.all_to_all(partial, "subj", 0, 0, tiled=True)
+    sent = call(add_pair, "add_pair", shape(stacked), keep, to_other_core(send))
+    received = lax.all_to_all(sent, "chip", 0, 0, tiled=True)
     scale = float(count * objects * obj)
     packed = call(
         lambda *refs: subject_grads(*refs, total=scale),
         "subject_grads",
         shape((obj, strips + 8, LANES)),
-        object_all,
+        own,
+        other,
         labels,
         left,
         carried,
@@ -225,21 +254,24 @@
 
 
 def solution(mesh):
+    subj, obj = mesh.shape["subj"], mesh.shape["obj"]
+    cores = Mesh(mesh.devices.reshape(subj // 2, 2, obj), ("chip", "core", "obj"))
+    rows = ("chip", "core")
     placed = (
-        P(("subj", "obj"), None),
-        P(("obj", "subj"), None),
-        P(None, "subj", "obj"),
-        P(None, "subj", "obj"),
+        P((*rows, "obj"), None),
+        P(("obj", *rows), None),
+        P(None, rows, "obj"),
+        P(None, rows, "obj"),
     )
     return jax.shard_map(
         body,
-        mesh=mesh,
+        mesh=cores,
         in_specs=placed,
         out_specs=(
-            P(("subj", "obj"), None),
-            P(("obj", "subj"), None),
-            P(None, "subj", "obj"),
-            P(("subj", "obj")),
+            P((*rows, "obj"), None),
+            P(("obj", *rows), None),
+            P(None, rows, "obj"),
+            P((*rows, "obj")),
         ),
         check_vma=False,
     )

time: 138 us -> 130 us (0.942)
  the two profiles are of different devices: /device:TPU:14 before, /device:TPU:8 now
where the time goes in v2:
time: 130 us
  blocking collectives  82.7 us (64%)
  Pallas kernels  26 us (20%)
  waiting for transfers between devices  10.3 us (8%)
  starting transfers between devices  7.5 us (6%)
  local copies, waits for them, and re-layouts  2.68 us (2%)
    all_to_all x1, blocking collectives, body(): subject_all = lax.all_to_all(sent, 'obj', 0, 0, tiled=True)  37.8 us
    all_to_all x1, blocking collectives, body(): received = lax.all_to_all(sent, 'obj', 0, 0, tiled=True)  29.4 us
    pallas_call x7, Pallas kernels, call(): pl.pallas_call(kernel, out_shape=outs, scratch_shapes=scratch, name=name)  26 us
    all_to_all x1, blocking collectives, body(): own = lax.all_to_all(sent, 'chip', 0, 0, tiled=True)  15.5 us
    all_to_all x1, waiting for transfers between devices, body(): received = lax.all_to_all(sent, 'chip', 0, 0, tiled=True)  5.68 us
    ppermute x2, waiting for transfers between devices, to_other_core(): return lax.ppermute(array, 'core', [(0, 1), (1, 0)])  4.58 us
    ppermute x2, starting transfers between devices, to_other_core(): return lax.ppermute(array, 'core', [(0, 1), (1, 0)])  3.95 us
    all_to_all x1, starting transfers between devices, body(): received = lax.all_to_all(sent, 'chip', 0, 0, tiled=True)  3.55 us
  transfers between devices with their start and end apart: 3, of which 3 were waited for; matrix products, arithmetic and copies ran while one was open for 0% of the time, Pallas kernels for 5%

profile of v2, /device:TPU:8, one launch (start us, length us, event | category | flops | bytes accessed | tf_op | source)
XLA Modules:
  0.0 129.8 jit_solution(4681860112769947752)
XLA Ops:
  0.6 1.7 %pack_subject.1 = bf16[32,72,128]{2,1,0:T(8,128)(2,1)} custom-call(bf16[16,512]{1,0:T(8,128)(2,1)} %subject_ref.1, bf16[2,16,32]{2,1,0:T(8,128)(2,1)} %bitcast.3), custom_call_target="tpu_custom_call" | custom-call | tf_op jit(solution)/shard_map/pack_subject/pallas_call | solution.py:188
  2.3 37.8 %all_to_all.20.gathered_ref.subject_ref = bf16[32,72,128]{2,1,0:T(8,128)(2,1)} all-to-all(bf16[32,72,128]{2,1,0:T(8,128)(2,1)} %pack_subject.1), channel_id=1, replica_groups=mesh['chip'=8,'core'=2,'obj'=32] {'obj'}, dimensions={0} | all-to-all | bytes 1179648 | tf_op jit(solution)/shard_map/all_to_all | solution.py:205
  40.1 2.1 %pack_object.1 = bf16[8,96,512]{2,1,0:T(8,128)(2,1)} custom-call(bf16[32,72,128]{2,1,0:T(8,128)(2,1)} %all_to_all.20.gathered_ref.subject_ref, bf16[32,512]{1,0:T(8,128)(2,1)} %object_ref.1), custom_call_target="tpu_custom_call" | custom-call | tf_op jit(solution)/shard_map/pack_object/pallas_call | solution.py:188
  42.2 15.5 %all_to_all.21.own_ref.refs_0_ = bf16[8,96,512]{2,1,0:T(8,128)(2,1)S(1)} all-to-all(bf16[8,96,512]{2,1,0:T(8,128)(2,1)} %pack_object.1), channel_id=1, replica_groups=mesh['chip'=8,'core'=2,'obj'=32] {'chip'}, dimensions={0} | all-to-all | bytes 1572864 | tf_op jit(solution)/shard_map/all_to_all | solution.py:208
  57.7 0.0 copy-start
  57.7 1.9 %collective-permute-start = (bf16[8,96,512]{2,1,0:T(8,128)(2,1)S(1)}, bf16[8,96,512]{2,1,0:T(8,128)(2,1)S(1)}, u32[]{:S(2)}, u32[]{:S(2)}) collective-permute-start(bf16[8,96,512]{2,1,0:T(8,128)(2,1)S(1)} %all_to_all.21.own_ref.refs_0_), channel_id=1, source_target_pairs={{0,32},{32,0},{1,33},{33,1},{2,34},{34,2},{3,35},{35,3},{4,36},{36... | collective-permute-start | bytes 2359304 | tf_op jit(solution)/shard_map/ppermute | solution.py:192
  59.6 2.3 %collective-permute-done.other_ref.refs_1_ = bf16[8,96,512]{2,1,0:T(8,128)(2,1)S(1)} collective-permute-done((bf16[8,96,512]{2,1,0:T(8,128)(2,1)S(1)}, bf16[8,96,512]{2,1,0:T(8,128)(2,1)S(1)}, u32[]{:S(2)}, u32[]{:S(2)}) %collective-permute-start) | collective-permute-done | bytes 786464 | tf_op jit(solution)/shard_map/ppermute | solution.py:192
  61.9 0.0 copy-done
  61.9 0.0 copy-start.1
  61.9 0.9 copy-done.1
  62.8 8.7 %grads.1 = (bf16[8,96,512]{2,1,0:T(8,128)(2,1)}, bf16[8,96,512]{2,1,0:T(8,128)(2,1)}, bf16[2,512,512]{2,1,0:T(8,128)(2,1)}, bf16[2,512,512]{2,1,0:T(8,128)(2,1)}) custom-call(bf16[32,72,128]{2,1,0:T(8,128)(2,1)} %all_to_all.20.gathered_ref.subject_ref, bf16[8,96,512]{2,1,0:T(8,128)(2,1)} %copy-done, bf16[8,96,512]{2,1,0:T(8,128)(2,1)} %copy-done.1, ...), custom_call_target="tpu_custom_call" | custom-call | tf_op jit(solution)/shard_map/grads/pallas_call | solution.py:188
  71.5 2.0 %collective-permute-start.1 = (bf16[8,96,512]{2,1,0:T(8,128)(2,1)}, bf16[8,96,512]{2,1,0:T(8,128)(2,1)S(1)}, u32[]{:S(2)}, u32[]{:S(2)}) collective-permute-start(bf16[8,96,512]{2,1,0:T(8,128)(2,1)} %get-tuple-element.14), channel_id=1, source_target_pairs={{0,32},{32,0},{1,33},{33,1},{2,34},{34,2},{3,35},{35,3},{4,36},{36... | collective-permute-start | bytes 2359304 | tf_op jit(solution)/shard_map/ppermute | solution.py:192
  73.5 2.3 %collective-permute-done.1.received_ref = bf16[8,96,512]{2,1,0:T(8,128)(2,1)S(1)} collective-permute-done((bf16[8,96,512]{2,1,0:T(8,128)(2,1)}, bf16[8,96,512]{2,1,0:T(8,128)(2,1)S(1)}, u32[]{:S(2)}, u32[]{:S(2)}) %collective-permute-start.1) | collective-permute-done | bytes 786464 | tf_op jit(solution)/shard_map/ppermute | solution.py:192
  75.8 0.0 copy-start.3
  75.8 0.9 copy-done.3
  76.8 2.4 %add_pair.1 = bf16[8,96,512]{2,1,0:T(8,128)(2,1)} custom-call(bf16[8,96,512]{2,1,0:T(8,128)(2,1)} %get-tuple-element.13.keep_ref, bf16[8,96,512]{2,1,0:T(8,128)(2,1)} %copy-done.3), custom_call_target="tpu_custom_call" | custom-call | tf_op jit(solution)/shard_map/add_pair/pallas_call | solution.py:188
  79.2 3.5 %all-to-all-start.2 = ((bf16[8,96,512]{2,1,0:T(8,128)(2,1)}), bf16[8,96,512]{2,1,0:T(8,128)(2,1)S(1)}, u32[]{:S(2)}, u32[]{:S(2)}) async-start(bf16[8,96,512]{2,1,0:T(8,128)(2,1)} %add_pair.1), calls=%async_computation.2 | async-start | bytes 1572864 | tf_op jit(solution)/shard_map/all_to_all | solution.py:222
  82.7 6.8 %subject_grads.1.subject_ref = bf16[32,72,128]{2,1,0:T(8,128)(2,1)} custom-call(bf16[8,96,512]{2,1,0:T(8,128)(2,1)} %copy-done, bf16[8,96,512]{2,1,0:T(8,128)(2,1)} %copy-done.1, s32[2,512,512]{2,1,0:T(8,128)} %refs_2_.1, bf16[2,512,512]{2,1,0:T(8,128)(2,1)} %get-tuple-element.15.refs_3_, bf16[2,512,512]{2,1,0:T(8,128)(2,1)} %get-tuple-element.16.refs_4_), custom_call_target="tpu_custom_call" | custom-call | tf_op jit(solution)/shard_map/subject_grads/pallas_call | solution.py:188
  89.5 5.7 %all-to-all-done.2.partial_ref = bf16[8,96,512]{2,1,0:T(8,128)(2,1)S(1)} async-done(((bf16[8,96,512]{2,1,0:T(8,128)(2,1)}), bf16[8,96,512]{2,1,0:T(8,128)(2,1)S(1)}, u32[]{:S(2)}, u32[]{:S(2)}) %all-to-all-start.2) | async-done | bytes 786464 | tf_op jit(solution)/shard_map/all_to_all | solution.py:222
  95.2 0.0 copy-start.2
  95.2 0.9 copy-done.2
  96.1 2.4 %sum_object.1 = (f32[32,512]{1,0:T(8,128)}, bf16[32,80,128]{2,1,0:T(8,128)(2,1)}) custom-call(bf16[8,96,512]{2,1,0:T(8,128)(2,1)} %copy-done.2, bf16[32,72,128]{2,1,0:T(8,128)(2,1)} %subject_grads.1.subject_ref), custom_call_target="tpu_custom_call" | custom-call | tf_op jit(solution)/shard_map/sum_object/pallas_call | solution.py:188
  98.5 29.4 %all_to_all.22.refs_0_ = bf16[32,80,128]{2,1,0:T(8,128)(2,1)} all-to-all(bf16[32,80,128]{2,1,0:T(8,128)(2,1)} %get-tuple-element.17), channel_id=1, replica_groups=mesh['chip'=8,'core'=2,'obj'=32] {'obj'}, dimensions={0} | all-to-all | bytes 1310720 | tf_op jit(solution)/shard_map/all_to_all | solution.py:241
  127.9 1.9 %sum_subject.1 = (f32[16,512]{1,0:T(8,128)}, f32[2,16,32]{2,1,0:T(8,128)}, f32[1,16]{1,0:T(1,128)}) custom-call(bf16[32,80,128]{2,1,0:T(8,128)(2,1)} %all_to_all.22.refs_0_), custom_call_target="tpu_custom_call" | custom-call | tf_op jit(solution)/shard_map/sum_subject/pallas_call | solution.py:188
Async XLA Ops:
  57.7 4.2 %copy-start = (bf16[8,96,512]{2,1,0:T(8,128)(2,1)}, bf16[8,96,512]{2,1,0:T(8,128)(2,1)S(1)}, u32[]{:S(2)}) copy-start(bf16[8,96,512]{2,1,0:T(8,128)(2,1)S(1)} %all_to_all.21.own_ref.refs_0_) | copy-start | bytes 2359300
  57.7 4.2 %collective-permute-start = (bf16[8,96,512]{2,1,0:T(8,128)(2,1)S(1)}, bf16[8,96,512]{2,1,0:T(8,128)(2,1)S(1)}, u32[]{:S(2)}, u32[]{:S(2)}) collective-permute-start(bf16[8,96,512]{2,1,0:T(8,128)(2,1)S(1)} %all_to_all.21.own_ref.refs_0_), channel_id=1, source_target_pairs={{0,32},{32,0},{1,33},{33,1},{2,34},{34,2},{3,35},{35,3},{4,36},{36... | collective-permute-start | bytes 2359304 | tf_op jit(solution)/shard_map/ppermute | solution.py:192
  61.9 0.9 copy-start.1
  71.5 4.4 %collective-permute-start.1 = (bf16[8,96,512]{2,1,0:T(8,128)(2,1)}, bf16[8,96,512]{2,1,0:T(8,128)(2,1)S(1)}, u32[]{:S(2)}, u32[]{:S(2)}) collective-permute-start(bf16[8,96,512]{2,1,0:T(8,128)(2,1)} %get-tuple-element.14), channel_id=1, source_target_pairs={{0,32},{32,0},{1,33},{33,1},{2,34},{34,2},{3,35},{35,3},{4,36},{36... | collective-permute-start | bytes 2359304 | tf_op jit(solution)/shard_map/ppermute | solution.py:192
  75.8 0.9 copy-start.3
  79.2 16.0 %all-to-all-start.2 = ((bf16[8,96,512]{2,1,0:T(8,128)(2,1)}), bf16[8,96,512]{2,1,0:T(8,128)(2,1)S(1)}, u32[]{:S(2)}, u32[]{:S(2)}) async-start(bf16[8,96,512]{2,1,0:T(8,128)(2,1)} %add_pair.1), calls=%async_computation.2 | async-start | bytes 1572864 | tf_op jit(solution)/shard_map/all_to_all | solution.py:222
  95.2 0.9 copy-start.2

commit v3 on v2

--- a/solution.py
+++ b/solution.py
@@ -10,6 +10,7 @@
 BF16 = jnp.bfloat16
 LANES = 128
 CHUNK = 128
+GRANT = 20 * 2**20
 
 
 def halves_to_lanes(rows):
@@ -185,7 +186,13 @@
 
 
 def call(kernel, name, outs, *args, scratch=()):
-    return pl.pallas_call(kernel, out_shape=outs, scratch_shapes=scratch, name=name)(*args)
+    return pl.pallas_call(
+        kernel,
+        out_shape=outs,
+        scratch_shapes=scratch,
+        name=name,
+        compiler_params=pltpu.CompilerParams(vmem_limit_bytes=GRANT),
+    )(*args)
 
 
 def to_other_core(array):

time: 130 us -> 122 us (0.938)
  Pallas kernels: 26 us -> 11.6 us
  local copies, waits for them, and re-layouts: 2.68 us -> 8.59 us
    pallas_call x7, Pallas kernels: 26 us -> 11.6 us  [call(): pl.pallas_call(kernel, out_shape=outs, scratch_shapes=scratch, name=name,...]
    unnamed x8 -> x22, local copies, waits for them, and re-layouts: 2.68 us -> 8.59 us
  transfers between devices with their start and end apart: 3 -> 3, of which waited for: 3 -> 3; matrix products, arithmetic and copies ran while one was open for 0% -> 0% of each run, Pallas kernels for 5% -> 3%
where the time goes in v3:
time: 122 us; the launch traced here: 121 us
  blocking collectives  82 us (67%)
  Pallas kernels  11.6 us (10%)
  waiting for transfers between devices  10.1 us (8%)
  local copies, waits for them, and re-layouts  8.59 us (7%)
  starting transfers between devices  8.15 us (7%)
    all_to_all x1, blocking collectives, body(): subject_all = lax.all_to_all(sent, 'obj', 0, 0, tiled=True)  37.6 us
    all_to_all x1, blocking collectives, body(): received = lax.all_to_all(sent, 'obj', 0, 0, tiled=True)  29.1 us
    all_to_all x1, blocking collectives, body(): own = lax.all_to_all(sent, 'chip', 0, 0, tiled=True)  15.3 us
    pallas_call x7, Pallas kernels, call(): pl.pallas_call(kernel, out_shape=outs, scratch_shapes=scratch, name=name,...  11.6 us
    unnamed x22, local copies, waits for them, and re-layouts  8.59 us
    all_to_all x1, waiting for transfers between devices, body(): received = lax.all_to_all(sent, 'chip', 0, 0, tiled=True)  5.68 us
    ppermute x2, waiting for transfers between devices, to_other_core(): return lax.ppermute(array, 'core', [(0, 1), (1, 0)])  4.37 us
    all_to_all x1, starting transfers between devices, body(): received = lax.all_to_all(sent, 'chip', 0, 0, tiled=True)  4.21 us
  transfers between devices with their start and end apart: 3, of which 3 were waited for; matrix products, arithmetic and copies ran while one was open for 0% of the time, Pallas kernels for 3%

profile of v3, /device:TPU:8, one launch (start us, length us, event | category | flops | bytes accessed | tf_op | source)
XLA Modules:
  0.0 121.1 jit_solution(7505041419460205018)
XLA Ops:
  0.6 0.0 copy-start.9
  0.6 0.7 copy-done.9
  1.3 0.0 copy-start.10
  1.4 0.7 copy-done.10
  2.0 0.1 pack_subject.1
  2.2 0.0 copy-start
  2.2 37.6 %all_to_all.20.gathered_ref.subject_ref = bf16[32,72,128]{2,1,0:T(8,128)(2,1)S(1)} all-to-all(bf16[32,72,128]{2,1,0:T(8,128)(2,1)S(1)} %pack_subject.1), channel_id=1, replica_groups=mesh['chip'=8,'core'=2,'obj'=32] {'obj'}, dimensions={0} | all-to-all | bytes 1179648 | tf_op jit(solution)/shard_map/all_to_all | solution.py:212
  39.9 0.0 copy-start.8
  39.9 0.8 copy-done.8
  40.6 0.2 pack_object.1
  40.8 15.3 %all_to_all.21.own_ref.refs_0_ = bf16[8,96,512]{2,1,0:T(8,128)(2,1)S(1)} all-to-all(bf16[8,96,512]{2,1,0:T(8,128)(2,1)S(1)} %pack_object.1), channel_id=1, replica_groups=mesh['chip'=8,'core'=2,'obj'=32] {'chip'}, dimensions={0} | all-to-all | bytes 1572864 | tf_op jit(solution)/shard_map/all_to_all | solution.py:215
  56.1 1.9 %collective-permute-start = (bf16[8,96,512]{2,1,0:T(8,128)(2,1)S(1)}, bf16[8,96,512]{2,1,0:T(8,128)(2,1)S(1)}, u32[]{:S(2)}, u32[]{:S(2)}) collective-permute-start(bf16[8,96,512]{2,1,0:T(8,128)(2,1)S(1)} %all_to_all.21.own_ref.refs_0_), channel_id=1, source_target_pairs={{0,32},{32,0},{1,33},{33,1},{2,34},{34,2},{3,35},{35,3},{4,36},{36... | collective-permute-start | bytes 2359304 | tf_op jit(solution)/shard_map/ppermute | solution.py:199
  58.0 2.3 %collective-permute-done.other_ref.refs_1_ = bf16[8,96,512]{2,1,0:T(8,128)(2,1)S(1)} collective-permute-done((bf16[8,96,512]{2,1,0:T(8,128)(2,1)S(1)}, bf16[8,96,512]{2,1,0:T(8,128)(2,1)S(1)}, u32[]{:S(2)}, u32[]{:S(2)}) %collective-permute-start) | collective-permute-done | bytes 786464 | tf_op jit(solution)/shard_map/ppermute | solution.py:199
  60.2 0.0 copy-done
  60.2 0.0 copy-start.1
  60.2 5.0 %grads.1 = (bf16[8,96,512]{2,1,0:T(8,128)(2,1)S(1)}, bf16[8,96,512]{2,1,0:T(8,128)(2,1)S(1)}, bf16[2,512,512]{2,1,0:T(8,128)(2,1)S(1)}, bf16[2,512,512]{2,1,0:T(8,128)(2,1)S(1)}) custom-call(bf16[32,72,128]{2,1,0:T(8,128)(2,1)S(1)} %all_to_all.20.gathered_ref.subject_ref, bf16[8,96,512]{2,1,0:T(8,128)(2,1)S(1)} %all_to_all.21.own_ref.refs_0_, ...), custom_call_target="tpu_custom_call" | custom-call | tf_op jit(solution)/shard_map/grads/pallas_call | solution.py:189
  65.2 0.0 copy-done.1
  65.2 0.0 copy-start.4
  65.2 1.0 copy-done.4
  66.2 0.0 copy-start.6
  66.2 1.0 copy-done.6
  67.2 2.0 %collective-permute-start.1 = (bf16[8,96,512]{2,1,0:T(8,128)(2,1)S(1)}, bf16[8,96,512]{2,1,0:T(8,128)(2,1)S(1)}, u32[]{:S(2)}, u32[]{:S(2)}) collective-permute-start(bf16[8,96,512]{2,1,0:T(8,128)(2,1)S(1)} %get-tuple-element.14), channel_id=1, source_target_pairs={{0,32},{32,0},{1,33},{33,1},{2,34},{34,2},{3,35},{35,3},{4,36},{36... | collective-permute-start | bytes 2359304 | tf_op jit(solution)/shard_map/ppermute | solution.py:199
  69.3 2.1 %collective-permute-done.1.received_ref = bf16[8,96,512]{2,1,0:T(8,128)(2,1)S(1)} collective-permute-done((bf16[8,96,512]{2,1,0:T(8,128)(2,1)S(1)}, bf16[8,96,512]{2,1,0:T(8,128)(2,1)S(1)}, u32[]{:S(2)}, u32[]{:S(2)}) %collective-permute-start.1) | collective-permute-done | bytes 786464 | tf_op jit(solution)/shard_map/ppermute | solution.py:199
  71.4 0.2 add_pair.1
  71.6 0.0 copy-start.3
  71.6 0.9 copy-done.3
  72.4 4.2 %all-to-all-start.2 = ((bf16[8,96,512]{2,1,0:T(8,128)(2,1)}), bf16[8,96,512]{2,1,0:T(8,128)(2,1)}, u32[]{:S(2)}, u32[]{:S(2)}) async-start(bf16[8,96,512]{2,1,0:T(8,128)(2,1)} %copy-done.3), calls=%async_computation.2 | async-start | bytes 1572864 | tf_op jit(solution)/shard_map/all_to_all | solution.py:229
  76.7 0.0 copy-start.2
  76.7 1.1 copy-done.2
  77.8 0.0 copy-start.5
  77.8 1.2 %copy-done.5 = bf16[2,512,512]{2,1,0:T(8,128)(2,1)S(1)} copy-done((bf16[2,512,512]{2,1,0:T(8,128)(2,1)S(1)}, bf16[2,512,512]{2,1,0:T(8,128)(2,1)}, u32[]{:S(2)}) %copy-start.5) | copy-done | bytes 1048600
  79.0 0.0 copy-start.7
  79.0 1.2 %copy-done.7 = bf16[2,512,512]{2,1,0:T(8,128)(2,1)S(1)} copy-done((bf16[2,512,512]{2,1,0:T(8,128)(2,1)S(1)}, bf16[2,512,512]{2,1,0:T(8,128)(2,1)}, u32[]{:S(2)}) %copy-start.7) | copy-done | bytes 1048600
  80.2 3.3 %subject_grads.1.subject_ref = bf16[32,72,128]{2,1,0:T(8,128)(2,1)S(1)} custom-call(bf16[8,96,512]{2,1,0:T(8,128)(2,1)S(1)} %all_to_all.21.own_ref.refs_0_, bf16[8,96,512]{2,1,0:T(8,128)(2,1)S(1)} %copy-done.2, s32[2,512,512]{2,1,0:T(8,128)S(1)} %copy-done, bf16[2,512,512]{2,1,0:T(8,128)(2,1)S(1)} %copy-done.5, bf16[2,512,512]{2,1,0:T(8,128)(2,1)S(1)} %copy-done.7), custom_call_target="tpu_custom_call" | custom-call | tf_op jit(solution)/shard_map/subject_grads/pallas_call | solution.py:189
  83.5 5.7 %all-to-all-done.2.partial_ref = bf16[8,96,512]{2,1,0:T(8,128)(2,1)} async-done(((bf16[8,96,512]{2,1,0:T(8,128)(2,1)}), bf16[8,96,512]{2,1,0:T(8,128)(2,1)}, u32[]{:S(2)}, u32[]{:S(2)}) %all-to-all-start.2) | async-done | bytes 786464 | tf_op jit(solution)/shard_map/all_to_all | solution.py:229
  89.2 2.0 %sum_object.1 = (f32[32,512]{1,0:T(8,128)}, bf16[32,80,128]{2,1,0:T(8,128)(2,1)S(1)}) custom-call(bf16[8,96,512]{2,1,0:T(8,128)(2,1)} %all-to-all-done.2.partial_ref, bf16[32,72,128]{2,1,0:T(8,128)(2,1)S(1)} %subject_grads.1.subject_ref), custom_call_target="tpu_custom_call" | custom-call | tf_op jit(solution)/shard_map/sum_object/pallas_call | solution.py:189
  91.2 29.1 %all_to_all.22.refs_0_ = bf16[32,80,128]{2,1,0:T(8,128)(2,1)S(1)} all-to-all(bf16[32,80,128]{2,1,0:T(8,128)(2,1)S(1)} %get-tuple-element.17), channel_id=1, replica_groups=mesh['chip'=8,'core'=2,'obj'=32] {'obj'}, dimensions={0} | all-to-all | bytes 1310720 | tf_op jit(solution)/shard_map/all_to_all | solution.py:248
  120.3 0.8 sum_subject.1
Async XLA Ops:
  0.6 0.7 copy-start.9
  1.3 0.7 copy-start.10
  2.2 58.0 %copy-start = (s32[2,512,512]{2,1,0:T(8,128)S(1)}, s32[2,512,512]{2,1,0:T(8,128)}, u32[]{:S(2)}) copy-start(s32[2,512,512]{2,1,0:T(8,128)} %refs_2_.1) | copy-start | bytes 6291460
  39.9 0.8 copy-start.8
  56.1 4.2 %collective-permute-start = (bf16[8,96,512]{2,1,0:T(8,128)(2,1)S(1)}, bf16[8,96,512]{2,1,0:T(8,128)(2,1)S(1)}, u32[]{:S(2)}, u32[]{:S(2)}) collective-permute-start(bf16[8,96,512]{2,1,0:T(8,128)(2,1)S(1)} %all_to_all.21.own_ref.refs_0_), channel_id=1, source_target_pairs={{0,32},{32,0},{1,33},{33,1},{2,34},{34,2},{3,35},{35,3},{4,36},{36... | collective-permute-start | bytes 2359304 | tf_op jit(solution)/shard_map/ppermute | solution.py:199
  60.2 5.0 %copy-start.1 = (bf16[8,96,512]{2,1,0:T(8,128)(2,1)}, bf16[8,96,512]{2,1,0:T(8,128)(2,1)S(1)}, u32[]{:S(2)}) copy-start(bf16[8,96,512]{2,1,0:T(8,128)(2,1)S(1)} %collective-permute-done.other_ref.refs_1_) | copy-start | bytes 2359300
  65.2 1.0 copy-start.4
  66.2 1.0 copy-start.6
  67.2 4.2 %collective-permute-start.1 = (bf16[8,96,512]{2,1,0:T(8,128)(2,1)S(1)}, bf16[8,96,512]{2,1,0:T(8,128)(2,1)S(1)}, u32[]{:S(2)}, u32[]{:S(2)}) collective-permute-start(bf16[8,96,512]{2,1,0:T(8,128)(2,1)S(1)} %get-tuple-element.14), channel_id=1, source_target_pairs={{0,32},{32,0},{1,33},{33,1},{2,34},{34,2},{3,35},{35,3},{4,36},{36... | collective-permute-start | bytes 2359304 | tf_op jit(solution)/shard_map/ppermute | solution.py:199
  71.6 0.9 copy-start.3
  72.4 16.8 %all-to-all-start.2 = ((bf16[8,96,512]{2,1,0:T(8,128)(2,1)}), bf16[8,96,512]{2,1,0:T(8,128)(2,1)}, u32[]{:S(2)}, u32[]{:S(2)}) async-start(bf16[8,96,512]{2,1,0:T(8,128)(2,1)} %copy-done.3), calls=%async_computation.2 | async-start | bytes 1572864 | tf_op jit(solution)/shard_map/all_to_all | solution.py:229
  76.7 1.1 copy-start.2
  77.8 1.2 %copy-start.5 = (bf16[2,512,512]{2,1,0:T(8,128)(2,1)S(1)}, bf16[2,512,512]{2,1,0:T(8,128)(2,1)}, u32[]{:S(2)}) copy-start(bf16[2,512,512]{2,1,0:T(8,128)(2,1)} %copy-done.4) | copy-start | bytes 3145732
  79.0 1.2 %copy-start.7 = (bf16[2,512,512]{2,1,0:T(8,128)(2,1)S(1)}, bf16[2,512,512]{2,1,0:T(8,128)(2,1)}, u32[]{:S(2)}) copy-start(bf16[2,512,512]{2,1,0:T(8,128)(2,1)} %copy-done.6) | copy-start | bytes 3145732

commit v4 on v3

--- a/solution.py
+++ b/solution.py
@@ -32,8 +32,19 @@
     return lax.dot_general(a, b, ((contract[:1], contract[1:]), ((), ())), preferred_element_type=F32)
 
 
-def pack_subject(subject_ref, relation_ref, out_ref):
+def pack_subject(
+    subject_hbm, relation_hbm, object_hbm, out_ref, object_ref, subject_ref, relation_ref, arrived
+):
     copies, _, _ = out_ref.shape
+    loads = [
+        pltpu.make_async_copy(subject_hbm, subject_ref, arrived.at[0]),
+        pltpu.make_async_copy(relation_hbm, relation_ref, arrived.at[1]),
+        pltpu.make_async_copy(object_hbm, object_ref, arrived.at[2]),
+    ]
+    for load in loads:
+        load.start()
+    for load in loads:
+        load.wait()
     turned = jnp.concatenate([relation_ref[0], relation_ref[1]], axis=1).astype(F32)
     tile = halves_to_lanes(turned[None])[0].astype(BF16)
     factors = columns_to_rows(subject_ref[...])
@@ -81,8 +92,9 @@
     labels_ref,
     keep_ref,
     send_ref,
+    carried_ref,
+    scores_ref,
     left_ref,
-    carried_ref,
     residual_ref,
 ):
     relations, size, _ = labels_ref.shape
@@ -103,6 +115,7 @@
         for at in range(0, size, CHUNK):
             span = pl.ds(at, CHUNK)
             scores = dot(left_ref[k, span], objects, (1, 1))
+            scores_ref[k, span] = scores
             codes = labels_ref[k, span]
             small = jnp.exp(-jnp.abs(scores))
             scale = 1.0 / (1.0 + small)
@@ -118,16 +131,15 @@
     store_owners(keep_ref, send_ref, 0, rows, grad_object)
 
 
-def add_pair(keep_ref, received_ref, out_ref):
+def add_pair(keep_ref, received_ref, _, out_ref):
     out_ref[...] = (keep_ref[...].astype(F32) + received_ref[...].astype(F32)).astype(BF16)
 
 
-def subject_grads(own_ref, other_ref, labels_ref, left_ref, carried_ref, out_ref, *, total):
+def subject_grads(own_ref, other_ref, labels_ref, scores_ref, carried_ref, out_ref, *, total):
     relations, size, _ = labels_ref.shape
     rows = size // (2 * own_ref.shape[0])
     owners = out_ref.shape[0]
     per_owner = size // owners
-    objects = stacked_rows(own_ref, other_ref, 0, rows)
     rels = [stacked_rows(own_ref, other_ref, k + 1, rows) for k in range(relations)]
     here = CHUNK // per_owner
     for at in range(0, size, CHUNK):
@@ -135,7 +147,7 @@
         loss = jnp.zeros((CHUNK, 1), F32)
         grad = jnp.zeros((CHUNK, size), F32)
         for k in range(relations):
-            scores = dot(left_ref[k, span], objects, (1, 1))
+            scores = scores_ref[k, span]
             codes = labels_ref[k, span]
             soft = jnp.maximum(scores, 0.0) + jnp.log1p(jnp.exp(-jnp.abs(scores)))
             cell = jnp.where(codes == 2, soft - scores, soft)
@@ -185,10 +197,16 @@
     return jax.ShapeDtypeStruct(dims, dtype)
 
 
-def call(kernel, name, outs, *args, scratch=()):
+def call(kernel, name, outs, *args, scratch=(), spaces=None):
+    spaces = spaces or [None] * len(args)
+    args = [
+        pltpu.with_memory_space_constraint(a, s) if s is pltpu.HBM else a
+        for a, s in zip(args, spaces)
+    ]
     return pl.pallas_call(
         kernel,
         out_shape=outs,
+        in_specs=[pl.BlockSpec(memory_space=space) for space in spaces],
         scratch_shapes=scratch,
         name=name,
         compiler_params=pltpu.CompilerParams(vmem_limit_bytes=GRANT),
@@ -208,25 +226,37 @@
     _, subjects, objects = labels.shape
     strips = width // LANES * subject_rows
     turned = jnp.swapaxes(relations, 1, 2)
-    sent = call(pack_subject, "pack_subject", shape((obj, strips + 8, LANES)), subject_factors, turned)
+    sent, object_own = call(
+        pack_subject,
+        "pack_subject",
+        (shape((obj, strips + 8, LANES)), shape(object_factors.shape)),
+        subject_factors,
+        turned,
+        object_factors,
+        scratch=[
+            pltpu.VMEM(subject_factors.shape, BF16),
+            pltpu.VMEM(turned.shape, BF16),
+            pltpu.SemaphoreType.DMA((3,)),
+        ],
+        spaces=[pltpu.HBM] * 3,
+    )
     subject_all = lax.all_to_all(sent, "obj", 0, 0, tiled=True)
     stacked = (chips, object_part + count * rel_rows, width)
-    sent = call(pack_object, "pack_object", shape(stacked), subject_all, object_factors)
+    sent = call(pack_object, "pack_object", shape(stacked), subject_all, object_own)
     own = lax.all_to_all(sent, "chip", 0, 0, tiled=True)
     other = to_other_core(own)
     square = (count, subjects, width)
-    keep, send, left, carried = call(
+    keep, send, carried, scores = call(
         grads,
         "grads",
-        (shape(stacked), shape(stacked), shape(square), shape(square)),
+        (shape(stacked), shape(stacked), shape(square), shape(labels.shape, F32)),
         subject_all,
         own,
         other,
         labels,
-        scratch=[pltpu.VMEM((count, subjects, objects), BF16)],
-    )
-    sent = call(add_pair, "add_pair", shape(stacked), keep, to_other_core(send))
-    received = lax.all_to_all(sent, "chip", 0, 0, tiled=True)
+        scratch=[pltpu.VMEM(square, BF16), pltpu.VMEM(labels.shape, BF16)],
+    )
+    swapped = to_other_core(send)
     scale = float(count * objects * obj)
     packed = call(
         lambda *refs: subject_grads(*refs, total=scale),
@@ -235,9 +265,19 @@
         own,
         other,
         labels,
-        left,
+        scores,
         carried,
     )
+    sent = call(
+        add_pair,
+        "add_pair",
+        shape(stacked),
+        keep,
+        swapped,
+        packed,
+        spaces=[None, None, pl.ANY],
+    )
+    received = lax.all_to_all(sent, "chip", 0, 0, tiled=True)
     grad_object, sent = call(
         sum_object,
         "sum_object",

time: 122 us -> 115 us (0.943)
  blocking collectives: 82 us -> 96.8 us
  local copies, waits for them, and re-layouts: 8.59 us -> 0.01 us
  waiting for transfers between devices: 10.1 us -> 2.25 us
  starting transfers between devices: 8.15 us -> 3.96 us
    all_to_all x0 -> x1, blocking collectives: none -> 16 us  [body(): received = lax.all_to_all(sent, 'chip', 0, 0, tiled=True)]
    unnamed x22 -> x2, local copies, waits for them, and re-layouts: 8.59 us -> 0.01 us
    all_to_all x1 -> x0, waiting for transfers between devices: 5.68 us -> none  [body(): received = lax.all_to_all(sent, 'chip', 0, 0, tiled=True)]
    all_to_all x1 -> x0, starting transfers between devices: 4.21 us -> none  [body(): received = lax.all_to_all(sent, 'chip', 0, 0, tiled=True)]
    ppermute x2, waiting for transfers between devices: 4.37 us -> 2.25 us  [to_other_core(): return lax.ppermute(array, 'core', [(0, 1), (1, 0)])]
  transfers between devices with their start and end apart: 3 -> 2, of which waited for: 3 -> 1; matrix products, arithmetic and copies ran while one was open for 0% -> 0% of each run, Pallas kernels for 3% -> 2%
where the time goes in v4:
time: 115 us; the launch traced here: 114 us
  blocking collectives  96.8 us (84%)
  Pallas kernels  10.7 us (9%)
  starting transfers between devices  3.96 us (3%)
  waiting for transfers between devices  2.25 us (2%)
    all_to_all x1, blocking collectives, body(): subject_all = lax.all_to_all(sent, 'obj', 0, 0, tiled=True)  37.5 us
    all_to_all x1, blocking collectives, body(): received = lax.all_to_all(sent, 'obj', 0, 0, tiled=True)  28.1 us
    all_to_all x1, blocking collectives, body(): received = lax.all_to_all(sent, 'chip', 0, 0, tiled=True)  16 us
    all_to_all x1, blocking collectives, body(): own = lax.all_to_all(sent, 'chip', 0, 0, tiled=True)  15.3 us
    pallas_call x7, Pallas kernels, call(): pl.pallas_call(kernel, out_shape=outs, in_specs=[pl.BlockSpec(memory_spac...  10.7 us
    ppermute x2, starting transfers between devices, to_other_core(): return lax.ppermute(array, 'core', [(0, 1), (1, 0)])  3.96 us
  transfers between devices with their start and end apart: 2, of which 1 were waited for; matrix products, arithmetic and copies ran while one was open for 0% of the time, Pallas kernels for 2%

profile of v4, /device:TPU:8, one launch (start us, length us, event | category | flops | bytes accessed | tf_op | source)
XLA Modules:
  0.0 114.4 jit_solution(16445831345890321816)
XLA Ops:
  0.6 0.0 copy-start
  0.6 1.1 pack_subject.1
  1.8 37.5 %all_to_all.20.gathered_ref.subject_ref = bf16[32,72,128]{2,1,0:T(8,128)(2,1)S(1)} all-to-all(bf16[32,72,128]{2,1,0:T(8,128)(2,1)S(1)} %get-tuple-element.15), channel_id=1, replica_groups=mesh['chip'=8,'core'=2,'obj'=32] {'obj'}, dimensions={0} | all-to-all | bytes 1179648 | tf_op jit(solution)/shard_map/all_to_all | solution.py:243
  39.3 0.2 pack_object.1
  39.5 15.3 %all_to_all.21.own_ref.refs_0_ = bf16[8,96,512]{2,1,0:T(8,128)(2,1)S(1)} all-to-all(bf16[8,96,512]{2,1,0:T(8,128)(2,1)S(1)} %pack_object.1), channel_id=1, replica_groups=mesh['chip'=8,'core'=2,'obj'=32] {'chip'}, dimensions={0} | all-to-all | bytes 1572864 | tf_op jit(solution)/shard_map/all_to_all | solution.py:246
  54.7 1.9 %collective-permute-start = (bf16[8,96,512]{2,1,0:T(8,128)(2,1)S(1)}, bf16[8,96,512]{2,1,0:T(8,128)(2,1)S(1)}, u32[]{:S(2)}, u32[]{:S(2)}) collective-permute-start(bf16[8,96,512]{2,1,0:T(8,128)(2,1)S(1)} %all_to_all.21.own_ref.refs_0_), channel_id=1, source_target_pairs={{0,32},{32,0},{1,33},{33,1},{2,34},{34,2},{3,35},{35,3},{4,36},{36... | collective-permute-start | bytes 2359304 | tf_op jit(solution)/shard_map/ppermute | solution.py:217
  56.6 2.3 %collective-permute-done.other_ref.refs_1_ = bf16[8,96,512]{2,1,0:T(8,128)(2,1)S(1)} collective-permute-done((bf16[8,96,512]{2,1,0:T(8,128)(2,1)S(1)}, bf16[8,96,512]{2,1,0:T(8,128)(2,1)S(1)}, u32[]{:S(2)}, u32[]{:S(2)}) %collective-permute-start) | collective-permute-done | bytes 786464 | tf_op jit(solution)/shard_map/ppermute | solution.py:217
  58.9 0.0 copy-done
  58.9 5.0 %grads.1 = (bf16[8,96,512]{2,1,0:T(8,128)(2,1)S(1)}, bf16[8,96,512]{2,1,0:T(8,128)(2,1)S(1)}, bf16[2,512,512]{2,1,0:T(8,128)(2,1)S(1)}, f32[2,512,512]{2,1,0:T(8,128)S(1)}) custom-call(bf16[32,72,128]{2,1,0:T(8,128)(2,1)S(1)} %all_to_all.20.gathered_ref.subject_ref, bf16[8,96,512]{2,1,0:T(8,128)(2,1)S(1)} %all_to_all.21.own_ref.refs_0_, ...), custom_call_target="tpu_custom_call" | custom-call | tf_op jit(solution)/shard_map/grads/pallas_call | solution.py:206
  63.9 2.0 %collective-permute-start.1 = (bf16[8,96,512]{2,1,0:T(8,128)(2,1)S(1)}, bf16[8,96,512]{2,1,0:T(8,128)(2,1)S(1)}, u32[]{:S(2)}, u32[]{:S(2)}) collective-permute-start(bf16[8,96,512]{2,1,0:T(8,128)(2,1)S(1)} %get-tuple-element.18), channel_id=1, source_target_pairs={{0,32},{32,0},{1,33},{33,1},{2,34},{34,2},{3,35},{35,3},{4,36},{36... | collective-permute-start | bytes 2359304 | tf_op jit(solution)/shard_map/ppermute | solution.py:217
  65.9 2.6 %subject_grads.1._.subject_ref = bf16[32,72,128]{2,1,0:T(8,128)(2,1)S(1)} custom-call(bf16[8,96,512]{2,1,0:T(8,128)(2,1)S(1)} %all_to_all.21.own_ref.refs_0_, bf16[8,96,512]{2,1,0:T(8,128)(2,1)S(1)} %collective-permute-done.other_ref.refs_1_, s32[2,512,512]{2,1,0:T(8,128)S(1)} %copy-done, f32[2,512,512]{2,1,0:T(8,128)S(1)} %get-tuple-element.19.refs_3_, ...), custom_call_target="tpu_custom_call" | custom-call | tf_op jit(solution)/shard_map/subject_grads/pallas_call | solution.py:206
  68.5 0.0 collective-permute-done.1.received_ref
  68.5 0.2 add_pair.1
  68.7 16.0 %all_to_all.22.partial_ref = bf16[8,96,512]{2,1,0:T(8,128)(2,1)S(1)} all-to-all(bf16[8,96,512]{2,1,0:T(8,128)(2,1)S(1)} %add_pair.1), channel_id=1, replica_groups=mesh['chip'=8,'core'=2,'obj'=32] {'chip'}, dimensions={0} | all-to-all | bytes 1572864 | tf_op jit(solution)/shard_map/all_to_all | solution.py:280
  84.7 0.8 sum_object.1
  85.5 28.1 %all_to_all.23.refs_0_ = bf16[32,80,128]{2,1,0:T(8,128)(2,1)S(1)} all-to-all(bf16[32,80,128]{2,1,0:T(8,128)(2,1)S(1)} %get-tuple-element.21), channel_id=1, replica_groups=mesh['chip'=8,'core'=2,'obj'=32] {'obj'}, dimensions={0} | all-to-all | bytes 1310720 | tf_op jit(solution)/shard_map/all_to_all | solution.py:288
  113.6 0.8 sum_subject.1
Async XLA Ops:
  0.6 58.3 %copy-start = (s32[2,512,512]{2,1,0:T(8,128)S(1)}, s32[2,512,512]{2,1,0:T(8,128)}, u32[]{:S(2)}) copy-start(s32[2,512,512]{2,1,0:T(8,128)} %refs_2_.1) | copy-start | bytes 6291460
  54.7 4.2 %collective-permute-start = (bf16[8,96,512]{2,1,0:T(8,128)(2,1)S(1)}, bf16[8,96,512]{2,1,0:T(8,128)(2,1)S(1)}, u32[]{:S(2)}, u32[]{:S(2)}) collective-permute-start(bf16[8,96,512]{2,1,0:T(8,128)(2,1)S(1)} %all_to_all.21.own_ref.refs_0_), channel_id=1, source_target_pairs={{0,32},{32,0},{1,33},{33,1},{2,34},{34,2},{3,35},{35,3},{4,36},{36... | collective-permute-start | bytes 2359304 | tf_op jit(solution)/shard_map/ppermute | solution.py:217
  63.9 4.7 %collective-permute-start.1 = (bf16[8,96,512]{2,1,0:T(8,128)(2,1)S(1)}, bf16[8,96,512]{2,1,0:T(8,128)(2,1)S(1)}, u32[]{:S(2)}, u32[]{:S(2)}) collective-permute-start(bf16[8,96,512]{2,1,0:T(8,128)(2,1)S(1)} %get-tuple-element.18), channel_id=1, source_target_pairs={{0,32},{32,0},{1,33},{33,1},{2,34},{34,2},{3,35},{35,3},{4,36},{36... | collective-permute-start | bytes 2359304 | tf_op jit(solution)/shard_map/ppermute | solution.py:217

commit v5 on v4

--- a/solution.py
+++ b/solution.py
@@ -9,7 +9,7 @@
 F32 = jnp.float32
 BF16 = jnp.bfloat16
 LANES = 128
-CHUNK = 128
+CHUNK = 512
 GRANT = 20 * 2**20
 
 
@@ -67,6 +67,12 @@
         out_ref[p, rows:] = rel
 
 
+def read_codes(labels_ref, _, sign_ref):
+    for k in range(labels_ref.shape[0]):
+        codes = labels_ref[k]
+        sign_ref[k] = jnp.where(codes == 2, -1.0, jnp.where(codes > 0, 1.0, 0.0))
+
+
 def stacked_rows(own_ref, other_ref, part, rows):
     first = lax.axis_index("core") == 0
     own = own_ref[:, rows * part : rows * (part + 1), :]
@@ -78,26 +84,26 @@
 
 def store_owners(keep_ref, send_ref, part, rows, values):
     first = lax.axis_index("core") == 0
-    by_core = values.reshape(keep_ref.shape[0], 2, rows, values.shape[1])
+    by_core = values.astype(BF16).reshape(keep_ref.shape[0], 2, rows, values.shape[1])
     even, odd = by_core[:, 0], by_core[:, 1]
     span = slice(rows * part, rows * (part + 1))
-    keep_ref[:, span, :] = jnp.where(first, even, odd).astype(BF16)
-    send_ref[:, span, :] = jnp.where(first, odd, even).astype(BF16)
+    keep_ref[:, span, :] = jnp.where(first, even, odd)
+    send_ref[:, span, :] = jnp.where(first, odd, even)
 
 
 def grads(
     subject_ref,
     own_ref,
     other_ref,
-    labels_ref,
+    sign_ref,
     keep_ref,
     send_ref,
     carried_ref,
-    scores_ref,
+    signed_ref,
     left_ref,
     residual_ref,
 ):
-    relations, size, _ = labels_ref.shape
+    relations, size, _ = sign_ref.shape
     rows = size // (2 * keep_ref.shape[0])
     owners = subject_ref.shape[0]
     per_owner = size // owners
@@ -109,21 +115,28 @@
         axis=1,
     )
     objects = stacked_rows(own_ref, other_ref, 0, rows)
+    rels = [stacked_rows(own_ref, other_ref, k + 1, rows) for k in range(relations)]
+    spans = [pl.ds(at, CHUNK) for at in range(0, size, CHUNK)]
+
+    def project(k, span):
+        left_ref[k, span] = dot(subject[span.start : span.start + CHUNK], rels[k], (1, 0)).astype(BF16)
+
+    def settle(k, span):
+        sign = sign_ref[k, span]
+        signed = dot(left_ref[k, span], objects, (1, 1)) * sign
+        signed_ref[k, span] = signed
+        small = jnp.exp(-jnp.abs(signed))
+        sigmoid = jnp.where(signed >= 0.0, 1.0, small) / (1.0 + small)
+        residual_ref[k, span] = (sigmoid * sign).astype(BF16)
+
+    def carry(k, span):
+        carried_ref[k, span] = dot(residual_ref[k, span], objects, (1, 0)).astype(BF16)
+
     for k in range(relations):
-        rel = stacked_rows(own_ref, other_ref, k + 1, rows)
-        left_ref[k] = dot(subject, rel, (1, 0)).astype(BF16)
-        for at in range(0, size, CHUNK):
-            span = pl.ds(at, CHUNK)
-            scores = dot(left_ref[k, span], objects, (1, 1))
-            scores_ref[k, span] = scores
-            codes = labels_ref[k, span]
-            small = jnp.exp(-jnp.abs(scores))
-            scale = 1.0 / (1.0 + small)
-            sigmoid = jnp.where(scores >= 0.0, scale, small * scale)
-            target = jnp.where(codes == 2, 1.0, 0.0)
-            residual = jnp.where(codes > 0, sigmoid - target, 0.0).astype(BF16)
-            residual_ref[k, span] = residual
-            carried_ref[k, span] = dot(residual, objects, (1, 0)).astype(BF16)
+        for step in (project, settle, carry):
+            for span in spans:
+                step(k, span)
+    for k in range(relations):
         store_owners(keep_ref, send_ref, k + 1, rows, dot(subject, carried_ref[k], (0, 0)))
     grad_object = dot(residual_ref[0], left_ref[0], (0, 0))
     for k in range(1, relations):
@@ -135,8 +148,10 @@
     out_ref[...] = (keep_ref[...].astype(F32) + received_ref[...].astype(F32)).astype(BF16)
 
 
-def subject_grads(own_ref, other_ref, labels_ref, scores_ref, carried_ref, out_ref, *, total):
-    relations, size, _ = labels_ref.shape
+def subject_grads(
+    own_ref, other_ref, signed_ref, sign_ref, carried_ref, out_ref, *, total
+):
+    relations, size, _ = signed_ref.shape
     rows = size // (2 * own_ref.shape[0])
     owners = out_ref.shape[0]
     per_owner = size // owners
@@ -147,11 +162,10 @@
         loss = jnp.zeros((CHUNK, 1), F32)
         grad = jnp.zeros((CHUNK, size), F32)
         for k in range(relations):
-            scores = scores_ref[k, span]
-            codes = labels_ref[k, span]
-            soft = jnp.maximum(scores, 0.0) + jnp.log1p(jnp.exp(-jnp.abs(scores)))
-            cell = jnp.where(codes == 2, soft - scores, soft)
-            loss = loss + jnp.sum(jnp.where(codes > 0, cell, 0.0), axis=1, keepdims=True)
+            signed = signed_ref[k, span]
+            cell = jnp.maximum(signed, 0.0) + jnp.log1p(jnp.exp(-jnp.abs(signed)))
+            counted = sign_ref[k, span] != 0.0
+            loss = loss + jnp.sum(jnp.where(counted, cell, 0.0), axis=1, keepdims=True)
             grad = grad + dot(carried_ref[k, span], rels[k], (1, 1))
         first = at // per_owner
         grad = grad.astype(BF16).reshape(here, per_owner, size)
@@ -245,15 +259,18 @@
     sent = call(pack_object, "pack_object", shape(stacked), subject_all, object_own)
     own = lax.all_to_all(sent, "chip", 0, 0, tiled=True)
     other = to_other_core(own)
+    sign = call(
+        read_codes, "read_codes", shape(labels.shape, F32), labels, own, spaces=[None, pl.ANY]
+    )
     square = (count, subjects, width)
-    keep, send, carried, scores = call(
+    keep, send, carried, signed = call(
         grads,
         "grads",
         (shape(stacked), shape(stacked), shape(square), shape(labels.shape, F32)),
         subject_all,
         own,
         other,
-        labels,
+        sign,
         scratch=[pltpu.VMEM(square, BF16), pltpu.VMEM(labels.shape, BF16)],
     )
     swapped = to_other_core(send)
@@ -264,8 +281,8 @@
         shape((obj, strips + 8, LANES)),
         own,
         other,
-        labels,
-        scores,
+        signed,
+        sign,
         carried,
     )
     sent = call(

time: 115 us -> 112 us (0.974)
  Pallas kernels: 10.7 us -> 8.42 us
    pallas_call x7 -> x8, Pallas kernels: 10.7 us -> 8.42 us  [call(): pl.pallas_call(kernel, out_shape=outs, in_specs=[pl.BlockSpec(memory_spac...]
  transfers between devices with their start and end apart: 2 -> 2, of which waited for: 1 -> 2; matrix products, arithmetic and copies ran while one was open for 0% -> 0% of each run, Pallas kernels for 2% -> 2%
where the time goes in v5:
time: 112 us
  blocking collectives  96.4 us (86%)
  Pallas kernels  8.42 us (8%)
  starting transfers between devices  3.95 us (4%)
  waiting for transfers between devices  2.37 us (2%)
    all_to_all x1, blocking collectives, body(): subject_all = lax.all_to_all(sent, 'obj', 0, 0, tiled=True)  37.5 us
    all_to_all x1, blocking collectives, body(): received = lax.all_to_all(sent, 'obj', 0, 0, tiled=True)  27.8 us
    all_to_all x1, blocking collectives, body(): received = lax.all_to_all(sent, 'chip', 0, 0, tiled=True)  15.8 us
    all_to_all x1, blocking collectives, body(): own = lax.all_to_all(sent, 'chip', 0, 0, tiled=True)  15.3 us
    pallas_call x8, Pallas kernels, call(): pl.pallas_call(kernel, out_shape=outs, in_specs=[pl.BlockSpec(memory_spac...  8.42 us
    ppermute x2, starting transfers between devices, to_other_core(): return lax.ppermute(array, 'core', [(0, 1), (1, 0)])  3.95 us
    ppermute x2, waiting for transfers between devices, to_other_core(): return lax.ppermute(array, 'core', [(0, 1), (1, 0)])  2.37 us
  transfers between devices with their start and end apart: 2, of which 2 were waited for; matrix products, arithmetic and copies ran while one was open for 0% of the time, Pallas kernels for 2%

profile of v5, /device:TPU:8, one launch (start us, length us, event | category | flops | bytes accessed | tf_op | source)
XLA Modules:
  0.0 111.8 jit_solution(642384737943028567)
XLA Ops:
  0.6 0.0 copy-start
  0.6 1.1 pack_subject.1
  1.8 37.5 %all_to_all.20.gathered_ref.subject_ref = bf16[32,72,128]{2,1,0:T(8,128)(2,1)S(1)} all-to-all(bf16[32,72,128]{2,1,0:T(8,128)(2,1)S(1)} %get-tuple-element.15), channel_id=1, replica_groups=mesh['chip'=8,'core'=2,'obj'=32] {'obj'}, dimensions={0} | all-to-all | bytes 1179648 | tf_op jit(solution)/shard_map/all_to_all | solution.py:257
  39.3 0.2 pack_object.1
  39.5 15.3 %all_to_all.21._.own_ref.refs_0_ = bf16[8,96,512]{2,1,0:T(8,128)(2,1)S(1)} all-to-all(bf16[8,96,512]{2,1,0:T(8,128)(2,1)S(1)} %pack_object.1), channel_id=1, replica_groups=mesh['chip'=8,'core'=2,'obj'=32] {'chip'}, dimensions={0} | all-to-all | bytes 1572864 | tf_op jit(solution)/shard_map/all_to_all | solution.py:260
  54.7 1.9 %collective-permute-start = (bf16[8,96,512]{2,1,0:T(8,128)(2,1)S(1)}, bf16[8,96,512]{2,1,0:T(8,128)(2,1)S(1)}, u32[]{:S(2)}, u32[]{:S(2)}) collective-permute-start(bf16[8,96,512]{2,1,0:T(8,128)(2,1)S(1)} %all_to_all.21._.own_ref.refs_0_), channel_id=1, source_target_pairs={{0,32},{32,0},{1,33},{33,1},{2,34},{34,2},{3,35},{35,3},{4,36},{36... | collective-permute-start | bytes 2359304 | tf_op jit(solution)/shard_map/ppermute | solution.py:231
  56.6 0.0 copy-done
  56.6 0.3 read_codes.1.sign_ref.refs_3_
  56.9 2.0 %collective-permute-done.other_ref.refs_1_ = bf16[8,96,512]{2,1,0:T(8,128)(2,1)S(1)} collective-permute-done((bf16[8,96,512]{2,1,0:T(8,128)(2,1)S(1)}, bf16[8,96,512]{2,1,0:T(8,128)(2,1)S(1)}, u32[]{:S(2)}, u32[]{:S(2)}) %collective-permute-start) | collective-permute-done | bytes 786464 | tf_op jit(solution)/shard_map/ppermute | solution.py:231
  58.9 3.4 %grads.1 = (bf16[8,96,512]{2,1,0:T(8,128)(2,1)S(1)}, bf16[8,96,512]{2,1,0:T(8,128)(2,1)S(1)}, bf16[2,512,512]{2,1,0:T(8,128)(2,1)S(1)}, f32[2,512,512]{2,1,0:T(8,128)S(1)}) custom-call(bf16[32,72,128]{2,1,0:T(8,128)(2,1)S(1)} %all_to_all.20.gathered_ref.subject_ref, bf16[8,96,512]{2,1,0:T(8,128)(2,1)S(1)} %all_to_all.21._.own_ref.refs_0_, ...), custom_call_target="tpu_custom_call" | custom-call | tf_op jit(solution)/shard_map/grads/pallas_call | solution.py:220
  62.3 2.0 %collective-permute-start.1 = (bf16[8,96,512]{2,1,0:T(8,128)(2,1)S(1)}, bf16[8,96,512]{2,1,0:T(8,128)(2,1)S(1)}, u32[]{:S(2)}, u32[]{:S(2)}) collective-permute-start(bf16[8,96,512]{2,1,0:T(8,128)(2,1)S(1)} %get-tuple-element.18), channel_id=1, source_target_pairs={{0,32},{32,0},{1,33},{33,1},{2,34},{34,2},{3,35},{35,3},{4,36},{36... | collective-permute-start | bytes 2359304 | tf_op jit(solution)/shard_map/ppermute | solution.py:231
  64.3 1.7 %subject_grads.1._.subject_ref = bf16[32,72,128]{2,1,0:T(8,128)(2,1)S(1)} custom-call(bf16[8,96,512]{2,1,0:T(8,128)(2,1)S(1)} %all_to_all.21._.own_ref.refs_0_, bf16[8,96,512]{2,1,0:T(8,128)(2,1)S(1)} %collective-permute-done.other_ref.refs_1_, f32[2,512,512]{2,1,0:T(8,128)S(1)} %get-tuple-element.19.refs_2_, f32[2,512,512]{2,1,0:T(8,128)S(1)} %read_codes.1.sign_ref.refs_3_, ...), custom_call_target="tpu_custom_call" | custom-call | tf_op jit(solution)/shard_map/subject_grads/pallas_call | solution.py:220
  66.0 0.4 collective-permute-done.1.received_ref
  66.4 0.2 add_pair.1
  66.6 15.8 %all_to_all.22.partial_ref = bf16[8,96,512]{2,1,0:T(8,128)(2,1)S(1)} all-to-all(bf16[8,96,512]{2,1,0:T(8,128)(2,1)S(1)} %add_pair.1), channel_id=1, replica_groups=mesh['chip'=8,'core'=2,'obj'=32] {'chip'}, dimensions={0} | all-to-all | bytes 1572864 | tf_op jit(solution)/shard_map/all_to_all | solution.py:297
  82.4 0.8 sum_object.1
  83.3 27.8 %all_to_all.23.refs_0_ = bf16[32,80,128]{2,1,0:T(8,128)(2,1)S(1)} all-to-all(bf16[32,80,128]{2,1,0:T(8,128)(2,1)S(1)} %get-tuple-element.21), channel_id=1, replica_groups=mesh['chip'=8,'core'=2,'obj'=32] {'obj'}, dimensions={0} | all-to-all | bytes 1310720 | tf_op jit(solution)/shard_map/all_to_all | solution.py:305
  111.1 0.8 sum_subject.1
Async XLA Ops:
  0.6 56.0 %copy-start = (s32[2,512,512]{2,1,0:T(8,128)S(1)}, s32[2,512,512]{2,1,0:T(8,128)}, u32[]{:S(2)}) copy-start(s32[2,512,512]{2,1,0:T(8,128)} %labels_ref.1) | copy-start | bytes 6291460
  54.7 4.2 %collective-permute-start = (bf16[8,96,512]{2,1,0:T(8,128)(2,1)S(1)}, bf16[8,96,512]{2,1,0:T(8,128)(2,1)S(1)}, u32[]{:S(2)}, u32[]{:S(2)}) collective-permute-start(bf16[8,96,512]{2,1,0:T(8,128)(2,1)S(1)} %all_to_all.21._.own_ref.refs_0_), channel_id=1, source_target_pairs={{0,32},{32,0},{1,33},{33,1},{2,34},{34,2},{3,35},{35,3},{4,36},{36... | collective-permute-start | bytes 2359304 | tf_op jit(solution)/shard_map/ppermute | solution.py:231
  62.3 4.2 %collective-permute-start.1 = (bf16[8,96,512]{2,1,0:T(8,128)(2,1)S(1)}, bf16[8,96,512]{2,1,0:T(8,128)(2,1)S(1)}, u32[]{:S(2)}, u32[]{:S(2)}) collective-permute-start(bf16[8,96,512]{2,1,0:T(8,128)(2,1)S(1)} %get-tuple-element.18), channel_id=1, source_target_pairs={{0,32},{32,0},{1,33},{33,1},{2,34},{34,2},{3,35},{35,3},{4,36},{36... | collective-permute-start | bytes 2359304 | tf_op jit(solution)/shard_map/ppermute | solution.py:231

commit v6 on v5

--- a/solution.py
+++ b/solution.py
@@ -11,6 +11,7 @@
 LANES = 128
 CHUNK = 512
 GRANT = 20 * 2**20
+PAIR = 2
 
 
 def halves_to_lanes(rows):
@@ -149,7 +150,7 @@
 
 
 def subject_grads(
-    own_ref, other_ref, signed_ref, sign_ref, carried_ref, out_ref, *, total
+    own_ref, other_ref, signed_ref, sign_ref, carried_ref, out_ref, loss_ref, *, total
 ):
     relations, size, _ = signed_ref.shape
     rows = size // (2 * own_ref.shape[0])
@@ -173,38 +174,48 @@
             out_ref[first : first + here, c * per_owner : (c + 1) * per_owner, :] = grad[
                 :, :, c * LANES : (c + 1) * LANES
             ]
-        part = jnp.broadcast_to(loss / total, (CHUNK, LANES // 2)).reshape(here, per_owner, -1)
-        split = size // LANES * per_owner
-        out_ref[first : first + here, split : split + 8, :] = halves_to_lanes(part).astype(BF16)
-
-
-def sum_object(partial_ref, subject_ref, grad_ref, out_ref):
-    rows = grad_ref.shape[0]
-    width = grad_ref.shape[1]
-    total = jnp.sum(partial_ref[...].astype(F32), axis=0)
-    grad_ref[...] = total[:rows]
-    turned = total[rows:].T
-    owners = subject_ref.shape[0]
+        part = jnp.broadcast_to(loss / total, (CHUNK, LANES)).reshape(here, per_owner, LANES)
+        entry = lax.broadcasted_iota(jnp.int32, part.shape, 1)
+        lane = lax.broadcasted_iota(jnp.int32, part.shape, 2)
+        loss_ref[first : first + here] = jnp.sum(jnp.where(entry == lane, part, 0.0), axis=1)
+
+
+def sum_relations(partial_ref, subject_ref, loss_ref, out_ref, *, rows):
+    width = partial_ref.shape[2]
+    total = jnp.sum(partial_ref[:, rows:, :].astype(F32), axis=0)
+    turned = total.T
+    owners, strips, _ = subject_ref.shape
     tiles = halves_to_lanes(turned.reshape(owners, width // owners, -1)).astype(BF16)
-    split = subject_ref.shape[1]
-    out_ref[:, :split, :] = subject_ref[...]
-    out_ref[:, split:, :] = tiles
-
-
-def sum_subject(partial_ref, grad_ref, relation_ref, loss_ref, *, total):
+    piece = strips + 8 + PAIR
+    for p in range(owners):
+        at = p * piece
+        out_ref[at : at + strips] = subject_ref[p]
+        out_ref[at + strips : at + strips + 8] = tiles[p]
+        row = jnp.broadcast_to(loss_ref[p : p + 1], (PAIR, LANES))
+        out_ref[at + strips + 8 : at + piece] = row.astype(BF16)
+
+
+def sum_factors(
+    partial_ref, object_ref, grad_ref, grad_object_ref, relation_ref, loss_ref, *, owners, total
+):
     rows, width = grad_ref.shape
-    summed = jnp.sum(partial_ref[...].astype(F32), axis=0)
+    grad_object_ref[...] = jnp.sum(
+        object_ref[:, : grad_object_ref.shape[0], :].astype(F32), axis=0
+    )
+    piece = partial_ref.shape[0] // owners
+    summed = partial_ref[:piece].astype(F32)
+    for p in range(1, owners):
+        summed = summed + partial_ref[p * piece : (p + 1) * piece].astype(F32)
     blocks = width // LANES
     grad_ref[...] = jnp.concatenate(
         [summed[c * rows : (c + 1) * rows] for c in range(blocks)], axis=1
     )
     at = blocks * rows
-    loss = lanes_to_halves(summed[None, at : at + 8])[0]
-    loss_ref[...] = loss.T[:1]
-    turned = lanes_to_halves(summed[None, at + 8 : at + 16])[0] * (1.0 / total)
+    turned = lanes_to_halves(summed[None, at : at + 8])[0] * (1.0 / total)
     columns = relation_ref.shape[2]
     for k in range(relation_ref.shape[0]):
         relation_ref[k] = turned[:, k * columns : (k + 1) * columns]
+    loss_ref[...] = summed[at + 8 : at + 9, :rows]
 
 
 def shape(dims, dtype=BF16):
@@ -275,10 +286,10 @@
     )
     swapped = to_other_core(send)
     scale = float(count * objects * obj)
-    packed = call(
+    packed, loss_rows = call(
         lambda *refs: subject_grads(*refs, total=scale),
         "subject_grads",
-        shape((obj, strips + 8, LANES)),
+        (shape((obj, strips, LANES)), shape((obj, LANES), F32)),
         own,
         other,
         signed,
@@ -294,25 +305,30 @@
         packed,
         spaces=[None, None, pl.ANY],
     )
-    received = lax.all_to_all(sent, "chip", 0, 0, tiled=True)
-    grad_object, sent = call(
-        sum_object,
-        "sum_object",
-        (shape((object_part, width), F32), shape((obj, strips + 16, LANES))),
-        received,
+    object_partial = lax.all_to_all(sent, "chip", 0, 0, tiled=True)
+    piece = strips + 8 + PAIR
+    sent = call(
+        lambda *refs: sum_relations(*refs, rows=object_part),
+        "sum_relations",
+        shape((obj * piece, LANES)),
+        object_partial,
         packed,
-    )
-    received = lax.all_to_all(sent, "obj", 0, 0, tiled=True)
+        loss_rows,
+    )
+    sent = sent.reshape(-1, PAIR, LANES)
+    received = lax.all_to_all(sent, "obj", 0, 0, tiled=True).reshape(-1, LANES)
     scale = float(subjects * subj)
-    grad_subject, grad_relations, loss = call(
-        lambda *refs: sum_subject(*refs, total=scale),
-        "sum_subject",
+    grad_subject, grad_object, grad_relations, loss = call(
+        lambda *refs: sum_factors(*refs, owners=obj, total=scale),
+        "sum_factors",
         (
             shape((subject_rows, width), F32),
+            shape((object_part, width), F32),
             shape((count, rel_columns, rel_rows), F32),
             shape((1, subject_rows), F32),
         ),
         received,
+        object_partial,
     )
     return grad_subject, grad_object, jnp.swapaxes(grad_relations, 1, 2), loss.reshape(subject_rows)
 

time: 112 us -> 111 us (level)
  blocking collectives: 96.4 us -> 95.2 us
    all_to_all x2, blocking collectives: 43.6 us -> 42.4 us  [the longest x1 26.6 us: body(): received = lax.all_to_all(sent, 'obj', 0, 0, tiled=True).reshape(-1, LANES)]
where the time goes in v6:
time: 111 us; the launch traced here: 110 us
  blocking collectives  95.2 us (86%)
  Pallas kernels  7.95 us (7%)
  starting transfers between devices  3.95 us (4%)
  waiting for transfers between devices  2.37 us (2%)
    all_to_all x1, blocking collectives, body(): subject_all = lax.all_to_all(sent, 'obj', 0, 0, tiled=True)  37.5 us
    all_to_all x1, blocking collectives, body(): received = lax.all_to_all(sent, 'obj', 0, 0, tiled=True).reshape(-1, LANES)  26.6 us
    all_to_all x1, blocking collectives, body(): object_partial = lax.all_to_all(sent, 'chip', 0, 0, tiled=True)  15.8 us
    all_to_all x1, blocking collectives, body(): own = lax.all_to_all(sent, 'chip', 0, 0, tiled=True)  15.3 us
    pallas_call x8, Pallas kernels, call(): pl.pallas_call(kernel, out_shape=outs, in_specs=[pl.BlockSpec(memory_spac...  7.95 us
    ppermute x2, starting transfers between devices, to_other_core(): return lax.ppermute(array, 'core', [(0, 1), (1, 0)])  3.95 us
    ppermute x2, waiting for transfers between devices, to_other_core(): return lax.ppermute(array, 'core', [(0, 1), (1, 0)])  2.37 us
  transfers between devices with their start and end apart: 2, of which 2 were waited for; matrix products, arithmetic and copies ran while one was open for 0% of the time, Pallas kernels for 2%

profile of v6, /device:TPU:8, one launch (start us, length us, event | category | flops | bytes accessed | tf_op | source)
XLA Modules:
  0.0 110.2 jit_solution(17726601576081187557)
XLA Ops:
  0.6 0.0 copy-start
  0.6 1.1 %pack_subject.1 = (bf16[32,72,128]{2,1,0:T(8,128)(2,1)S(1)}, bf16[32,512]{1,0:T(8,128)(2,1)S(1)}) custom-call(bf16[16,512]{1,0:T(8,128)(2,1)} %subject_hbm.1, bf16[2,16,32]{2,1,0:T(8,128)(2,1)} %bitcast.7, bf16[32,512]{1,0:T(8,128)(2,1)} %object_hbm.1), custom_call_target="tpu_custom_call" | custom-call | tf_op jit(solution)/shard_map/pack_subject/pallas_call | solution.py:231
  1.8 37.5 %all_to_all.20.gathered_ref.subject_ref = bf16[32,72,128]{2,1,0:T(8,128)(2,1)S(1)} all-to-all(bf16[32,72,128]{2,1,0:T(8,128)(2,1)S(1)} %get-tuple-element.16), channel_id=1, replica_groups=mesh['chip'=8,'core'=2,'obj'=32] {'obj'}, dimensions={0} | all-to-all | bytes 1179648 | tf_op jit(solution)/shard_map/all_to_all | solution.py:268
  39.3 0.2 pack_object.1
  39.5 15.3 %all_to_all.21._.own_ref.refs_0_ = bf16[8,96,512]{2,1,0:T(8,128)(2,1)S(1)} all-to-all(bf16[8,96,512]{2,1,0:T(8,128)(2,1)S(1)} %pack_object.1), channel_id=1, replica_groups=mesh['chip'=8,'core'=2,'obj'=32] {'chip'}, dimensions={0} | all-to-all | bytes 1572864 | tf_op jit(solution)/shard_map/all_to_all | solution.py:271
  54.7 1.9 %collective-permute-start = (bf16[8,96,512]{2,1,0:T(8,128)(2,1)S(1)}, bf16[8,96,512]{2,1,0:T(8,128)(2,1)S(1)}, u32[]{:S(2)}, u32[]{:S(2)}) collective-permute-start(bf16[8,96,512]{2,1,0:T(8,128)(2,1)S(1)} %all_to_all.21._.own_ref.refs_0_), channel_id=1, source_target_pairs={{0,32},{32,0},{1,33},{33,1},{2,34},{34,2},{3,35},{35,3},{4,36},{36... | collective-permute-start | bytes 2359304 | tf_op jit(solution)/shard_map/ppermute | solution.py:242
  56.6 0.0 copy-done
  56.6 0.3 read_codes.1.sign_ref.refs_3_
  56.9 2.0 %collective-permute-done.other_ref.refs_1_ = bf16[8,96,512]{2,1,0:T(8,128)(2,1)S(1)} collective-permute-done((bf16[8,96,512]{2,1,0:T(8,128)(2,1)S(1)}, bf16[8,96,512]{2,1,0:T(8,128)(2,1)S(1)}, u32[]{:S(2)}, u32[]{:S(2)}) %collective-permute-start) | collective-permute-done | bytes 786464 | tf_op jit(solution)/shard_map/ppermute | solution.py:242
  58.9 3.4 %grads.1 = (bf16[8,96,512]{2,1,0:T(8,128)(2,1)S(1)}, bf16[8,96,512]{2,1,0:T(8,128)(2,1)S(1)}, bf16[2,512,512]{2,1,0:T(8,128)(2,1)S(1)}, f32[2,512,512]{2,1,0:T(8,128)S(1)}) custom-call(bf16[32,72,128]{2,1,0:T(8,128)(2,1)S(1)} %all_to_all.20.gathered_ref.subject_ref, bf16[8,96,512]{2,1,0:T(8,128)(2,1)S(1)} %all_to_all.21._.own_ref.refs_0_, ...), custom_call_target="tpu_custom_call" | custom-call | tf_op jit(solution)/shard_map/grads/pallas_call | solution.py:231
  62.3 2.0 %collective-permute-start.1 = (bf16[8,96,512]{2,1,0:T(8,128)(2,1)S(1)}, bf16[8,96,512]{2,1,0:T(8,128)(2,1)S(1)}, u32[]{:S(2)}, u32[]{:S(2)}) collective-permute-start(bf16[8,96,512]{2,1,0:T(8,128)(2,1)S(1)} %get-tuple-element.19), channel_id=1, source_target_pairs={{0,32},{32,0},{1,33},{33,1},{2,34},{34,2},{3,35},{35,3},{4,36},{36... | collective-permute-start | bytes 2359304 | tf_op jit(solution)/shard_map/ppermute | solution.py:242
  64.3 1.7 %subject_grads.1 = (bf16[32,64,128]{2,1,0:T(8,128)(2,1)S(1)}, f32[32,128]{1,0:T(8,128)S(1)}) custom-call(bf16[8,96,512]{2,1,0:T(8,128)(2,1)S(1)} %all_to_all.21._.own_ref.refs_0_, bf16[8,96,512]{2,1,0:T(8,128)(2,1)S(1)} %collective-permute-done.other_ref.refs_1_, f32[2,512,512]{2,1,0:T(8,128)S(1)} %get-tuple-element.20.refs_2_, ...), custom_call_target="tpu_custom_call" | custom-call | tf_op jit(solution)/shard_map/subject_grads/pallas_call | solution.py:231
  66.0 0.4 collective-permute-done.1.received_ref
  66.4 0.2 add_pair.1
  66.6 15.8 %all_to_all.22.refs_0_.refs_1_ = bf16[8,96,512]{2,1,0:T(8,128)(2,1)S(1)} all-to-all(bf16[8,96,512]{2,1,0:T(8,128)(2,1)S(1)} %add_pair.1), channel_id=1, replica_groups=mesh['chip'=8,'core'=2,'obj'=32] {'chip'}, dimensions={0} | all-to-all | bytes 1572864 | tf_op jit(solution)/shard_map/all_to_all | solution.py:308
  82.4 0.3 sum_relations.1
  82.8 26.6 %all_to_all.23 = bf16[1184,2,128]{2,1,0:T(2,128)(2,1)S(1)} all-to-all(bf16[1184,2,128]{2,1,0:T(2,128)(2,1)S(1)} %bitcast.6), channel_id=1, replica_groups=mesh['chip'=8,'core'=2,'obj'=32] {'obj'}, dimensions={0} | all-to-all | bytes 1212416 | tf_op jit(solution)/shard_map/all_to_all | solution.py:319
  109.4 0.8 sum_factors.1
Async XLA Ops:
  0.6 56.0 %copy-start = (s32[2,512,512]{2,1,0:T(8,128)S(1)}, s32[2,512,512]{2,1,0:T(8,128)}, u32[]{:S(2)}) copy-start(s32[2,512,512]{2,1,0:T(8,128)} %labels_ref.1) | copy-start | bytes 6291460
  54.7 4.2 %collective-permute-start = (bf16[8,96,512]{2,1,0:T(8,128)(2,1)S(1)}, bf16[8,96,512]{2,1,0:T(8,128)(2,1)S(1)}, u32[]{:S(2)}, u32[]{:S(2)}) collective-permute-start(bf16[8,96,512]{2,1,0:T(8,128)(2,1)S(1)} %all_to_all.21._.own_ref.refs_0_), channel_id=1, source_target_pairs={{0,32},{32,0},{1,33},{33,1},{2,34},{34,2},{3,35},{35,3},{4,36},{36... | collective-permute-start | bytes 2359304 | tf_op jit(solution)/shard_map/ppermute | solution.py:242
  62.3 4.2 %collective-permute-start.1 = (bf16[8,96,512]{2,1,0:T(8,128)(2,1)S(1)}, bf16[8,96,512]{2,1,0:T(8,128)(2,1)S(1)}, u32[]{:S(2)}, u32[]{:S(2)}) collective-permute-start(bf16[8,96,512]{2,1,0:T(8,128)(2,1)S(1)} %get-tuple-element.19), channel_id=1, source_target_pairs={{0,32},{32,0},{1,33},{33,1},{2,34},{34,2},{3,35},{35,3},{4,36},{36... | collective-permute-start | bytes 2359304 | tf_op jit(solution)/shard_map/ppermute | solution.py:242

commit v7 on v6

--- a/solution.py
+++ b/solution.py
@@ -117,28 +117,34 @@
     )
     objects = stacked_rows(own_ref, other_ref, 0, rows)
     rels = [stacked_rows(own_ref, other_ref, k + 1, rows) for k in range(relations)]
-    spans = [pl.ds(at, CHUNK) for at in range(0, size, CHUNK)]
-
-    def project(k, span):
-        left_ref[k, span] = dot(subject[span.start : span.start + CHUNK], rels[k], (1, 0)).astype(BF16)
-
-    def settle(k, span):
-        sign = sign_ref[k, span]
-        signed = dot(left_ref[k, span], objects, (1, 1)) * sign
-        signed_ref[k, span] = signed
+
+    def project(k):
+        left_ref[k] = dot(subject, rels[k], (1, 0)).astype(BF16)
+
+    def score(k):
+        signed_ref[k] = dot(left_ref[k], objects, (1, 1))
+
+    def settle(k):
+        sign = sign_ref[k]
+        signed = signed_ref[k] * sign
         small = jnp.exp(-jnp.abs(signed))
         sigmoid = jnp.where(signed >= 0.0, 1.0, small) / (1.0 + small)
-        residual_ref[k, span] = (sigmoid * sign).astype(BF16)
-
-    def carry(k, span):
-        carried_ref[k, span] = dot(residual_ref[k, span], objects, (1, 0)).astype(BF16)
+        residual_ref[k] = (sigmoid * sign).astype(BF16)
+
+    def carry(k):
+        carried_ref[k] = dot(residual_ref[k], objects, (1, 0)).astype(BF16)
+
+    def relation_grad(k):
+        store_owners(keep_ref, send_ref, k + 1, rows, dot(subject, carried_ref[k], (0, 0)))
 
     for k in range(relations):
-        for step in (project, settle, carry):
-            for span in spans:
-                step(k, span)
-    for k in range(relations):
-        store_owners(keep_ref, send_ref, k + 1, rows, dot(subject, carried_ref[k], (0, 0)))
+        project(k)
+        score(k)
+        settle(k)
+        if k > 0:
+            relation_grad(k - 1)
+        carry(k)
+    relation_grad(relations - 1)
     grad_object = dot(residual_ref[0], left_ref[0], (0, 0))
     for k in range(1, relations):
         grad_object = grad_object + dot(residual_ref[k], left_ref[k], (0, 0))
@@ -163,9 +169,10 @@
         loss = jnp.zeros((CHUNK, 1), F32)
         grad = jnp.zeros((CHUNK, size), F32)
         for k in range(relations):
-            signed = signed_ref[k, span]
+            sign = sign_ref[k, span]
+            signed = signed_ref[k, span] * sign
             cell = jnp.maximum(signed, 0.0) + jnp.log1p(jnp.exp(-jnp.abs(signed)))
-            counted = sign_ref[k, span] != 0.0
+            counted = sign != 0.0
             loss = loss + jnp.sum(jnp.where(counted, cell, 0.0), axis=1, keepdims=True)
             grad = grad + dot(carried_ref[k, span], rels[k], (1, 1))
         first = at // per_owner

time: 111 us -> 110 us (level)
  no operation moved by 1% of the time
where the time goes in v7:
time: 110 us
  blocking collectives  95.2 us (87%)
  Pallas kernels  7.82 us (7%)
  starting transfers between devices  3.95 us (4%)
  waiting for transfers between devices  2.31 us (2%)
    all_to_all x1, blocking collectives, body(): subject_all = lax.all_to_all(sent, 'obj', 0, 0, tiled=True)  37.5 us
    all_to_all x1, blocking collectives, body(): received = lax.all_to_all(sent, 'obj', 0, 0, tiled=True).reshape(-1, LANES)  26.6 us
    all_to_all x1, blocking collectives, body(): object_partial = lax.all_to_all(sent, 'chip', 0, 0, tiled=True)  15.8 us
    all_to_all x1, blocking collectives, body(): own = lax.all_to_all(sent, 'chip', 0, 0, tiled=True)  15.3 us
    pallas_call x8, Pallas kernels, call(): pl.pallas_call(kernel, out_shape=outs, in_specs=[pl.BlockSpec(memory_spac...  7.82 us
    ppermute x2, starting transfers between devices, to_other_core(): return lax.ppermute(array, 'core', [(0, 1), (1, 0)])  3.95 us
    ppermute x2, waiting for transfers between devices, to_other_core(): return lax.ppermute(array, 'core', [(0, 1), (1, 0)])  2.31 us
  transfers between devices with their start and end apart: 2, of which 2 were waited for; matrix products, arithmetic and copies ran while one was open for 0% of the time, Pallas kernels for 2%

profile of v7, /device:TPU:8, one launch (start us, length us, event | category | flops | bytes accessed | tf_op | source)
XLA Modules:
  0.0 110.0 jit_solution(5483014482329609317)
XLA Ops:
  0.6 0.0 copy-start
  0.6 1.1 %pack_subject.1 = (bf16[32,72,128]{2,1,0:T(8,128)(2,1)S(1)}, bf16[32,512]{1,0:T(8,128)(2,1)S(1)}) custom-call(bf16[16,512]{1,0:T(8,128)(2,1)} %subject_hbm.1, bf16[2,16,32]{2,1,0:T(8,128)(2,1)} %bitcast.7, bf16[32,512]{1,0:T(8,128)(2,1)} %object_hbm.1), custom_call_target="tpu_custom_call" | custom-call | tf_op jit(solution)/shard_map/pack_subject/pallas_call | solution.py:238
  1.8 37.5 %all_to_all.20.gathered_ref.subject_ref = bf16[32,72,128]{2,1,0:T(8,128)(2,1)S(1)} all-to-all(bf16[32,72,128]{2,1,0:T(8,128)(2,1)S(1)} %get-tuple-element.16), channel_id=1, replica_groups=mesh['chip'=8,'core'=2,'obj'=32] {'obj'}, dimensions={0} | all-to-all | bytes 1179648 | tf_op jit(solution)/shard_map/all_to_all | solution.py:275
  39.3 0.2 pack_object.1
  39.5 15.3 %all_to_all.21._.own_ref.refs_0_ = bf16[8,96,512]{2,1,0:T(8,128)(2,1)S(1)} all-to-all(bf16[8,96,512]{2,1,0:T(8,128)(2,1)S(1)} %pack_object.1), channel_id=1, replica_groups=mesh['chip'=8,'core'=2,'obj'=32] {'chip'}, dimensions={0} | all-to-all | bytes 1572864 | tf_op jit(solution)/shard_map/all_to_all | solution.py:278
  54.7 1.9 %collective-permute-start = (bf16[8,96,512]{2,1,0:T(8,128)(2,1)S(1)}, bf16[8,96,512]{2,1,0:T(8,128)(2,1)S(1)}, u32[]{:S(2)}, u32[]{:S(2)}) collective-permute-start(bf16[8,96,512]{2,1,0:T(8,128)(2,1)S(1)} %all_to_all.21._.own_ref.refs_0_), channel_id=1, source_target_pairs={{0,32},{32,0},{1,33},{33,1},{2,34},{34,2},{3,35},{35,3},{4,36},{36... | collective-permute-start | bytes 2359304 | tf_op jit(solution)/shard_map/ppermute | solution.py:249
  56.6 0.0 copy-done
  56.6 0.3 read_codes.1.sign_ref.refs_3_
  56.9 2.0 %collective-permute-done.other_ref.refs_1_ = bf16[8,96,512]{2,1,0:T(8,128)(2,1)S(1)} collective-permute-done((bf16[8,96,512]{2,1,0:T(8,128)(2,1)S(1)}, bf16[8,96,512]{2,1,0:T(8,128)(2,1)S(1)}, u32[]{:S(2)}, u32[]{:S(2)}) %collective-permute-start) | collective-permute-done | bytes 786464 | tf_op jit(solution)/shard_map/ppermute | solution.py:249
  58.9 3.2 %grads.1 = (bf16[8,96,512]{2,1,0:T(8,128)(2,1)S(1)}, bf16[8,96,512]{2,1,0:T(8,128)(2,1)S(1)}, bf16[2,512,512]{2,1,0:T(8,128)(2,1)S(1)}, f32[2,512,512]{2,1,0:T(8,128)S(1)}) custom-call(bf16[32,72,128]{2,1,0:T(8,128)(2,1)S(1)} %all_to_all.20.gathered_ref.subject_ref, bf16[8,96,512]{2,1,0:T(8,128)(2,1)S(1)} %all_to_all.21._.own_ref.refs_0_, ...), custom_call_target="tpu_custom_call" | custom-call | tf_op jit(solution)/shard_map/grads/pallas_call | solution.py:238
  62.1 2.0 %collective-permute-start.1 = (bf16[8,96,512]{2,1,0:T(8,128)(2,1)S(1)}, bf16[8,96,512]{2,1,0:T(8,128)(2,1)S(1)}, u32[]{:S(2)}, u32[]{:S(2)}) collective-permute-start(bf16[8,96,512]{2,1,0:T(8,128)(2,1)S(1)} %get-tuple-element.19), channel_id=1, source_target_pairs={{0,32},{32,0},{1,33},{33,1},{2,34},{34,2},{3,35},{35,3},{4,36},{36... | collective-permute-start | bytes 2359304 | tf_op jit(solution)/shard_map/ppermute | solution.py:249
  64.1 1.8 %subject_grads.1 = (bf16[32,64,128]{2,1,0:T(8,128)(2,1)S(1)}, f32[32,128]{1,0:T(8,128)S(1)}) custom-call(bf16[8,96,512]{2,1,0:T(8,128)(2,1)S(1)} %all_to_all.21._.own_ref.refs_0_, bf16[8,96,512]{2,1,0:T(8,128)(2,1)S(1)} %collective-permute-done.other_ref.refs_1_, f32[2,512,512]{2,1,0:T(8,128)S(1)} %get-tuple-element.20.refs_2_, ...), custom_call_target="tpu_custom_call" | custom-call | tf_op jit(solution)/shard_map/subject_grads/pallas_call | solution.py:238
  65.9 0.3 collective-permute-done.1.received_ref
  66.2 0.2 add_pair.1
  66.4 15.8 %all_to_all.22.refs_0_.refs_1_ = bf16[8,96,512]{2,1,0:T(8,128)(2,1)S(1)} all-to-all(bf16[8,96,512]{2,1,0:T(8,128)(2,1)S(1)} %add_pair.1), channel_id=1, replica_groups=mesh['chip'=8,'core'=2,'obj'=32] {'chip'}, dimensions={0} | all-to-all | bytes 1572864 | tf_op jit(solution)/shard_map/all_to_all | solution.py:315
  82.3 0.3 sum_relations.1
  82.6 26.6 %all_to_all.23 = bf16[1184,2,128]{2,1,0:T(2,128)(2,1)S(1)} all-to-all(bf16[1184,2,128]{2,1,0:T(2,128)(2,1)S(1)} %bitcast.6), channel_id=1, replica_groups=mesh['chip'=8,'core'=2,'obj'=32] {'obj'}, dimensions={0} | all-to-all | bytes 1212416 | tf_op jit(solution)/shard_map/all_to_all | solution.py:326
  109.2 0.8 sum_factors.1
Async XLA Ops:
  0.6 56.0 %copy-start = (s32[2,512,512]{2,1,0:T(8,128)S(1)}, s32[2,512,512]{2,1,0:T(8,128)}, u32[]{:S(2)}) copy-start(s32[2,512,512]{2,1,0:T(8,128)} %labels_ref.1) | copy-start | bytes 6291460
  54.7 4.2 %collective-permute-start = (bf16[8,96,512]{2,1,0:T(8,128)(2,1)S(1)}, bf16[8,96,512]{2,1,0:T(8,128)(2,1)S(1)}, u32[]{:S(2)}, u32[]{:S(2)}) collective-permute-start(bf16[8,96,512]{2,1,0:T(8,128)(2,1)S(1)} %all_to_all.21._.own_ref.refs_0_), channel_id=1, source_target_pairs={{0,32},{32,0},{1,33},{33,1},{2,34},{34,2},{3,35},{35,3},{4,36},{36... | collective-permute-start | bytes 2359304 | tf_op jit(solution)/shard_map/ppermute | solution.py:249
  62.1 4.2 %collective-permute-start.1 = (bf16[8,96,512]{2,1,0:T(8,128)(2,1)S(1)}, bf16[8,96,512]{2,1,0:T(8,128)(2,1)S(1)}, u32[]{:S(2)}, u32[]{:S(2)}) collective-permute-start(bf16[8,96,512]{2,1,0:T(8,128)(2,1)S(1)} %get-tuple-element.19), channel_id=1, source_target_pairs={{0,32},{32,0},{1,33},{33,1},{2,34},{34,2},{3,35},{35,3},{4,36},{36... | collective-permute-start | bytes 2359304 | tf_op jit(solution)/shard_map/ppermute | solution.py:249

commit v8 on v7

--- a/solution.py
+++ b/solution.py
@@ -44,7 +44,7 @@
     ]
     for load in loads:
         load.start()
-    for load in loads:
+    for load in loads[:2]:
         load.wait()
     turned = jnp.concatenate([relation_ref[0], relation_ref[1]], axis=1).astype(F32)
     tile = halves_to_lanes(turned[None])[0].astype(BF16)
@@ -53,6 +53,7 @@
     for p in range(copies):
         out_ref[p, :split] = factors
         out_ref[p, split:] = tile
+    loads[2].wait()
 
 
 def pack_object(gathered_ref, object_ref, out_ref):
@@ -68,8 +69,16 @@
         out_ref[p, rows:] = rel
 
 
-def read_codes(labels_ref, _, sign_ref):
-    for k in range(labels_ref.shape[0]):
+def read_codes(labels_hbm, _, sign_ref, labels_ref, arrived):
+    relations = labels_ref.shape[0]
+    loads = [
+        pltpu.make_async_copy(labels_hbm.at[k], labels_ref.at[k], arrived.at[k])
+        for k in range(relations)
+    ]
+    for load in loads:
+        load.start()
+    for k in range(relations):
+        loads[k].wait()
         codes = labels_ref[k]
         sign_ref[k] = jnp.where(codes == 2, -1.0, jnp.where(codes > 0, 1.0, 0.0))
 
@@ -278,7 +287,13 @@
     own = lax.all_to_all(sent, "chip", 0, 0, tiled=True)
     other = to_other_core(own)
     sign = call(
-        read_codes, "read_codes", shape(labels.shape, F32), labels, own, spaces=[None, pl.ANY]
+        read_codes,
+        "read_codes",
+        shape(labels.shape, F32),
+        labels,
+        own,
+        scratch=[pltpu.VMEM(labels.shape, labels.dtype), pltpu.SemaphoreType.DMA((count,))],
+        spaces=[pltpu.HBM, pl.ANY],
     )
     square = (count, subjects, width)
     keep, send, carried, signed = call(

time: 110 us -> 110 us (level)
  waiting for transfers between devices: 2.31 us -> 0.89 us
  Pallas kernels: 7.82 us -> 9.03 us
    ppermute x2, waiting for transfers between devices: 2.31 us -> 0.89 us  [to_other_core(): return lax.ppermute(array, 'core', [(0, 1), (1, 0)])]
    pallas_call x8, Pallas kernels: 7.82 us -> 9.03 us  [call(): pl.pallas_call(kernel, out_shape=outs, in_specs=[pl.BlockSpec(memory_spac...]
  transfers between devices with their start and end apart: 2 -> 2, of which waited for: 2 -> 2; matrix products, arithmetic and copies ran while one was open for 0% -> 0% of each run, Pallas kernels for 2% -> 3%
where the time goes in v8:
time: 110 us
  blocking collectives  95.2 us (87%)
  Pallas kernels  9.03 us (8%)
  starting transfers between devices  3.95 us (4%)
    all_to_all x1, blocking collectives, body(): subject_all = lax.all_to_all(sent, 'obj', 0, 0, tiled=True)  37.5 us
    all_to_all x1, blocking collectives, body(): received = lax.all_to_all(sent, 'obj', 0, 0, tiled=True).reshape(-1, LANES)  26.6 us
    all_to_all x1, blocking collectives, body(): object_partial = lax.all_to_all(sent, 'chip', 0, 0, tiled=True)  15.8 us
    all_to_all x1, blocking collectives, body(): own = lax.all_to_all(sent, 'chip', 0, 0, tiled=True)  15.3 us
    pallas_call x8, Pallas kernels, call(): pl.pallas_call(kernel, out_shape=outs, in_specs=[pl.BlockSpec(memory_spac...  9.03 us
    ppermute x2, starting transfers between devices, to_other_core(): return lax.ppermute(array, 'core', [(0, 1), (1, 0)])  3.95 us
  transfers between devices with their start and end apart: 2, of which 2 were waited for; matrix products, arithmetic and copies ran while one was open for 0% of the time, Pallas kernels for 3%

profile of v8, /device:TPU:8, one launch (start us, length us, event | category | flops | bytes accessed | tf_op | source)
XLA Modules:
  0.0 109.8 jit_solution(3658382653822804413)
XLA Ops:
  0.6 0.9 pack_subject.1
  1.5 37.5 %all_to_all.20.gathered_ref.subject_ref = bf16[32,72,128]{2,1,0:T(8,128)(2,1)S(1)} all-to-all(bf16[32,72,128]{2,1,0:T(8,128)(2,1)S(1)} %get-tuple-element.16), channel_id=1, replica_groups=mesh['chip'=8,'core'=2,'obj'=32] {'obj'}, dimensions={0} | all-to-all | bytes 1179648 | tf_op jit(solution)/shard_map/all_to_all | solution.py:284
  39.0 0.2 pack_object.1
  39.2 15.3 %all_to_all.21._.own_ref.refs_0_ = bf16[8,96,512]{2,1,0:T(8,128)(2,1)S(1)} all-to-all(bf16[8,96,512]{2,1,0:T(8,128)(2,1)S(1)} %pack_object.1), channel_id=1, replica_groups=mesh['chip'=8,'core'=2,'obj'=32] {'chip'}, dimensions={0} | all-to-all | bytes 1572864 | tf_op jit(solution)/shard_map/all_to_all | solution.py:287
  54.5 1.9 %collective-permute-start = (bf16[8,96,512]{2,1,0:T(8,128)(2,1)S(1)}, bf16[8,96,512]{2,1,0:T(8,128)(2,1)S(1)}, u32[]{:S(2)}, u32[]{:S(2)}) collective-permute-start(bf16[8,96,512]{2,1,0:T(8,128)(2,1)S(1)} %all_to_all.21._.own_ref.refs_0_), channel_id=1, source_target_pairs={{0,32},{32,0},{1,33},{33,1},{2,34},{34,2},{3,35},{35,3},{4,36},{36... | collective-permute-start | bytes 2359304 | tf_op jit(solution)/shard_map/ppermute | solution.py:258
  56.4 1.7 %read_codes.1.sign_ref.refs_3_ = f32[2,512,512]{2,1,0:T(8,128)S(1)} custom-call(s32[2,512,512]{2,1,0:T(8,128)} %labels_hbm.1, bf16[8,96,512]{2,1,0:T(8,128)(2,1)S(1)} %all_to_all.21._.own_ref.refs_0_), custom_call_target="tpu_custom_call" | custom-call | tf_op jit(solution)/shard_map/read_codes/pallas_call | solution.py:247
  58.1 0.5 collective-permute-done.other_ref.refs_1_
  58.7 3.2 %grads.1 = (bf16[8,96,512]{2,1,0:T(8,128)(2,1)S(1)}, bf16[8,96,512]{2,1,0:T(8,128)(2,1)S(1)}, bf16[2,512,512]{2,1,0:T(8,128)(2,1)S(1)}, f32[2,512,512]{2,1,0:T(8,128)S(1)}) custom-call(bf16[32,72,128]{2,1,0:T(8,128)(2,1)S(1)} %all_to_all.20.gathered_ref.subject_ref, bf16[8,96,512]{2,1,0:T(8,128)(2,1)S(1)} %all_to_all.21._.own_ref.refs_0_, ...), custom_call_target="tpu_custom_call" | custom-call | tf_op jit(solution)/shard_map/grads/pallas_call | solution.py:247
  61.8 2.0 %collective-permute-start.1 = (bf16[8,96,512]{2,1,0:T(8,128)(2,1)S(1)}, bf16[8,96,512]{2,1,0:T(8,128)(2,1)S(1)}, u32[]{:S(2)}, u32[]{:S(2)}) collective-permute-start(bf16[8,96,512]{2,1,0:T(8,128)(2,1)S(1)} %get-tuple-element.19), channel_id=1, source_target_pairs={{0,32},{32,0},{1,33},{33,1},{2,34},{34,2},{3,35},{35,3},{4,36},{36... | collective-permute-start | bytes 2359304 | tf_op jit(solution)/shard_map/ppermute | solution.py:258
  63.9 1.8 %subject_grads.1 = (bf16[32,64,128]{2,1,0:T(8,128)(2,1)S(1)}, f32[32,128]{1,0:T(8,128)S(1)}) custom-call(bf16[8,96,512]{2,1,0:T(8,128)(2,1)S(1)} %all_to_all.21._.own_ref.refs_0_, bf16[8,96,512]{2,1,0:T(8,128)(2,1)S(1)} %collective-permute-done.other_ref.refs_1_, f32[2,512,512]{2,1,0:T(8,128)S(1)} %get-tuple-element.20.refs_2_, ...), custom_call_target="tpu_custom_call" | custom-call | tf_op jit(solution)/shard_map/subject_grads/pallas_call | solution.py:247
  65.7 0.3 collective-permute-done.1.received_ref
  66.0 0.2 add_pair.1
  66.2 15.8 %all_to_all.22.refs_0_.refs_1_ = bf16[8,96,512]{2,1,0:T(8,128)(2,1)S(1)} all-to-all(bf16[8,96,512]{2,1,0:T(8,128)(2,1)S(1)} %add_pair.1), channel_id=1, replica_groups=mesh['chip'=8,'core'=2,'obj'=32] {'chip'}, dimensions={0} | all-to-all | bytes 1572864 | tf_op jit(solution)/shard_map/all_to_all | solution.py:330
  82.0 0.3 sum_relations.1
  82.3 26.6 %all_to_all.23 = bf16[1184,2,128]{2,1,0:T(2,128)(2,1)S(1)} all-to-all(bf16[1184,2,128]{2,1,0:T(2,128)(2,1)S(1)} %bitcast.6), channel_id=1, replica_groups=mesh['chip'=8,'core'=2,'obj'=32] {'obj'}, dimensions={0} | all-to-all | bytes 1212416 | tf_op jit(solution)/shard_map/all_to_all | solution.py:341
  108.9 0.8 sum_factors.1
Async XLA Ops:
  54.5 4.2 %collective-permute-start = (bf16[8,96,512]{2,1,0:T(8,128)(2,1)S(1)}, bf16[8,96,512]{2,1,0:T(8,128)(2,1)S(1)}, u32[]{:S(2)}, u32[]{:S(2)}) collective-permute-start(bf16[8,96,512]{2,1,0:T(8,128)(2,1)S(1)} %all_to_all.21._.own_ref.refs_0_), channel_id=1, source_target_pairs={{0,32},{32,0},{1,33},{33,1},{2,34},{34,2},{3,35},{35,3},{4,36},{36... | collective-permute-start | bytes 2359304 | tf_op jit(solution)/shard_map/ppermute | solution.py:258
  61.8 4.2 %collective-permute-start.1 = (bf16[8,96,512]{2,1,0:T(8,128)(2,1)S(1)}, bf16[8,96,512]{2,1,0:T(8,128)(2,1)S(1)}, u32[]{:S(2)}, u32[]{:S(2)}) collective-permute-start(bf16[8,96,512]{2,1,0:T(8,128)(2,1)S(1)} %get-tuple-element.19), channel_id=1, source_target_pairs={{0,32},{32,0},{1,33},{33,1},{2,34},{34,2},{3,35},{35,3},{4,36},{36... | collective-permute-start | bytes 2359304 | tf_op jit(solution)/shard_map/ppermute | solution.py:258

commit v9 on v8

--- a/solution.py
+++ b/solution.py
@@ -26,6 +26,30 @@
 def columns_to_rows(block):
     return jnp.concatenate(
         [block[:, c : c + LANES] for c in range(0, block.shape[1], LANES)], axis=0
+    )
+
+
+def by_core(block, rows):
+    runs = [block[:, c : c + rows] for c in range(0, block.shape[1], rows)]
+    return jnp.concatenate(runs[::2] + runs[1::2], axis=1)
+
+
+def in_order(block, rows):
+    half = block.shape[1] // 2
+    runs = []
+    for c in range(0, half, rows):
+        runs += [block[:, c : c + rows], block[:, half + c : half + c + rows]]
+    return jnp.concatenate(runs, axis=1)
+
+
+def subject_block(subject_ref, size):
+    per_owner = size // subject_ref.shape[0]
+    return jnp.concatenate(
+        [
+            subject_ref[:, c * per_owner : (c + 1) * per_owner, :].reshape(size, LANES)
+            for c in range(size // LANES)
+        ],
+        axis=1,
     )
 
 
@@ -48,7 +72,9 @@
         load.wait()
     turned = jnp.concatenate([relation_ref[0], relation_ref[1]], axis=1).astype(F32)
     tile = halves_to_lanes(turned[None])[0].astype(BF16)
-    factors = columns_to_rows(subject_ref[...])
+    rows = relation_ref.shape[2]
+    ordered = by_core(subject_ref[...].astype(F32), rows).astype(BF16)
+    factors = columns_to_rows(ordered)
     split = factors.shape[0]
     for p in range(copies):
         out_ref[p, :split] = factors
@@ -69,18 +95,29 @@
         out_ref[p, rows:] = rel
 
 
-def read_codes(labels_hbm, _, sign_ref, labels_ref, arrived):
-    relations = labels_ref.shape[0]
+def read_codes(labels_hbm, subject_ref, own_ref, sign_ref, half_ref, labels_ref, arrived):
+    relations, size, _ = labels_ref.shape
     loads = [
         pltpu.make_async_copy(labels_hbm.at[k], labels_ref.at[k], arrived.at[k])
         for k in range(relations)
     ]
     for load in loads:
         load.start()
+    subject = subject_block(subject_ref, size)
+    half = size // 2
+    ours = jnp.where(lax.axis_index("core") == 0, subject[:, :half], subject[:, half:])
+    rows = size // (2 * own_ref.shape[0])
+    for k in range(relations):
+        half_ref[k] = dot(ours, relation_half(own_ref, k, rows), (1, 0))
     for k in range(relations):
         loads[k].wait()
         codes = labels_ref[k]
         sign_ref[k] = jnp.where(codes == 2, -1.0, jnp.where(codes > 0, 1.0, 0.0))
+
+
+def relation_half(half_ref, relation, rows):
+    part = half_ref[:, rows * (relation + 1) : rows * (relation + 2), :]
+    return part.reshape(-1, part.shape[2])
 
 
 def stacked_rows(own_ref, other_ref, part, rows):
@@ -92,10 +129,9 @@
     return jnp.stack([even, odd], axis=1).reshape(-1, own.shape[2])
 
 
-def store_owners(keep_ref, send_ref, part, rows, values):
+def store_owners(keep_ref, send_ref, part, even, odd):
     first = lax.axis_index("core") == 0
-    by_core = values.astype(BF16).reshape(keep_ref.shape[0], 2, rows, values.shape[1])
-    even, odd = by_core[:, 0], by_core[:, 1]
+    rows = even.shape[1]
     span = slice(rows * part, rows * (part + 1))
     keep_ref[:, span, :] = jnp.where(first, even, odd)
     send_ref[:, span, :] = jnp.where(first, odd, even)
@@ -106,6 +142,7 @@
     own_ref,
     other_ref,
     sign_ref,
+    half_ref,
     keep_ref,
     send_ref,
     carried_ref,
@@ -115,20 +152,14 @@
 ):
     relations, size, _ = sign_ref.shape
     rows = size // (2 * keep_ref.shape[0])
-    owners = subject_ref.shape[0]
-    per_owner = size // owners
-    subject = jnp.concatenate(
-        [
-            subject_ref[:, c * per_owner : (c + 1) * per_owner, :].reshape(size, LANES)
-            for c in range(size // LANES)
-        ],
-        axis=1,
-    )
+    subject = subject_block(subject_ref, size)
+    half = size // 2
+    theirs = jnp.where(lax.axis_index("core") == 0, subject[:, half:], subject[:, :half])
     objects = stacked_rows(own_ref, other_ref, 0, rows)
-    rels = [stacked_rows(own_ref, other_ref, k + 1, rows) for k in range(relations)]
 
     def project(k):
-        left_ref[k] = dot(subject, rels[k], (1, 0)).astype(BF16)
+        rest = dot(theirs, relation_half(other_ref, k, rows), (1, 0))
+        left_ref[k] = (half_ref[k] + rest).astype(BF16)
 
     def score(k):
         signed_ref[k] = dot(left_ref[k], objects, (1, 1))
@@ -144,7 +175,8 @@
         carried_ref[k] = dot(residual_ref[k], objects, (1, 0)).astype(BF16)
 
     def relation_grad(k):
-        store_owners(keep_ref, send_ref, k + 1, rows, dot(subject, carried_ref[k], (0, 0)))
+        grad = dot(subject, carried_ref[k], (0, 0)).astype(BF16).reshape(2, -1, rows, size)
+        store_owners(keep_ref, send_ref, k + 1, grad[0], grad[1])
 
     for k in range(relations):
         project(k)
@@ -157,7 +189,8 @@
     grad_object = dot(residual_ref[0], left_ref[0], (0, 0))
     for k in range(1, relations):
         grad_object = grad_object + dot(residual_ref[k], left_ref[k], (0, 0))
-    store_owners(keep_ref, send_ref, 0, rows, grad_object)
+    owned = grad_object.astype(BF16).reshape(-1, 2, rows, size)
+    store_owners(keep_ref, send_ref, 0, owned[:, 0], owned[:, 1])
 
 
 def add_pair(keep_ref, received_ref, _, out_ref):
@@ -171,7 +204,12 @@
     rows = size // (2 * own_ref.shape[0])
     owners = out_ref.shape[0]
     per_owner = size // owners
-    rels = [stacked_rows(own_ref, other_ref, k + 1, rows) for k in range(relations)]
+    first_core = lax.axis_index("core") == 0
+    rels = []
+    for k in range(relations):
+        own, other = relation_half(own_ref, k, rows), relation_half(other_ref, k, rows)
+        even, odd = jnp.where(first_core, own, other), jnp.where(first_core, other, own)
+        rels.append(jnp.concatenate([even, odd], axis=0))
     here = CHUNK // per_owner
     for at in range(0, size, CHUNK):
         span = pl.ds(at, CHUNK)
@@ -223,9 +261,8 @@
     for p in range(1, owners):
         summed = summed + partial_ref[p * piece : (p + 1) * piece].astype(F32)
     blocks = width // LANES
-    grad_ref[...] = jnp.concatenate(
-        [summed[c * rows : (c + 1) * rows] for c in range(blocks)], axis=1
-    )
+    grad = jnp.concatenate([summed[c * rows : (c + 1) * rows] for c in range(blocks)], axis=1)
+    grad_ref[...] = in_order(grad, relation_ref.shape[2])
     at = blocks * rows
     turned = lanes_to_halves(summed[None, at : at + 8])[0] * (1.0 / total)
     columns = relation_ref.shape[2]
@@ -286,16 +323,17 @@
     sent = call(pack_object, "pack_object", shape(stacked), subject_all, object_own)
     own = lax.all_to_all(sent, "chip", 0, 0, tiled=True)
     other = to_other_core(own)
-    sign = call(
+    square = (count, subjects, width)
+    sign, half = call(
         read_codes,
         "read_codes",
-        shape(labels.shape, F32),
+        (shape(labels.shape, F32), shape(square, F32)),
         labels,
+        subject_all,
         own,
         scratch=[pltpu.VMEM(labels.shape, labels.dtype), pltpu.SemaphoreType.DMA((count,))],
-        spaces=[pltpu.HBM, pl.ANY],
-    )
-    square = (count, subjects, width)
+        spaces=[pltpu.HBM, None, None],
+    )
     keep, send, carried, signed = call(
         grads,
         "grads",
@@ -304,6 +342,7 @@
         own,
         other,
         sign,
+        half,
         scratch=[pltpu.VMEM(square, BF16), pltpu.VMEM(labels.shape, BF16)],
     )
     swapped = to_other_core(send)

time: 110 us -> 110 us (level)
  no operation moved by 1% of the time
where the time goes in v9:
time: 110 us
  blocking collectives  95.2 us (87%)
  Pallas kernels  8.76 us (8%)
  starting transfers between devices  3.95 us (4%)
    all_to_all x1, blocking collectives, body(): subject_all = lax.all_to_all(sent, 'obj', 0, 0, tiled=True)  37.5 us
    all_to_all x1, blocking collectives, body(): received = lax.all_to_all(sent, 'obj', 0, 0, tiled=True).reshape(-1, LANES)  26.6 us
    all_to_all x1, blocking collectives, body(): object_partial = lax.all_to_all(sent, 'chip', 0, 0, tiled=True)  15.8 us
    all_to_all x1, blocking collectives, body(): own = lax.all_to_all(sent, 'chip', 0, 0, tiled=True)  15.3 us
    pallas_call x8, Pallas kernels, call(): pl.pallas_call(kernel, out_shape=outs, in_specs=[pl.BlockSpec(memory_spac...  8.76 us
    ppermute x2, starting transfers between devices, to_other_core(): return lax.ppermute(array, 'core', [(0, 1), (1, 0)])  3.95 us
  transfers between devices with their start and end apart: 2, of which 2 were waited for; matrix products, arithmetic and copies ran while one was open for 0% of the time, Pallas kernels for 3%

profile of v9, /device:TPU:8, one launch (start us, length us, event | category | flops | bytes accessed | tf_op | source)
XLA Modules:
  0.0 109.5 jit_solution(5146838906788089636)
XLA Ops:
  0.6 0.9 pack_subject.1
  1.5 37.5 %all_to_all.20.gathered_ref.subject_ref = bf16[32,72,128]{2,1,0:T(8,128)(2,1)S(1)} all-to-all(bf16[32,72,128]{2,1,0:T(8,128)(2,1)S(1)} %get-tuple-element.18), channel_id=1, replica_groups=mesh['chip'=8,'core'=2,'obj'=32] {'obj'}, dimensions={0} | all-to-all | bytes 1179648 | tf_op jit(solution)/shard_map/all_to_all | solution.py:321
  39.0 0.2 pack_object.1
  39.2 15.3 %all_to_all.21.own_ref.refs_0_ = bf16[8,96,512]{2,1,0:T(8,128)(2,1)S(1)} all-to-all(bf16[8,96,512]{2,1,0:T(8,128)(2,1)S(1)} %pack_object.1), channel_id=1, replica_groups=mesh['chip'=8,'core'=2,'obj'=32] {'chip'}, dimensions={0} | all-to-all | bytes 1572864 | tf_op jit(solution)/shard_map/all_to_all | solution.py:324
  54.5 1.9 %collective-permute-start = (bf16[8,96,512]{2,1,0:T(8,128)(2,1)S(1)}, bf16[8,96,512]{2,1,0:T(8,128)(2,1)S(1)}, u32[]{:S(2)}, u32[]{:S(2)}) collective-permute-start(bf16[8,96,512]{2,1,0:T(8,128)(2,1)S(1)} %all_to_all.21.own_ref.refs_0_), channel_id=1, source_target_pairs={{0,32},{32,0},{1,33},{33,1},{2,34},{34,2},{3,35},{35,3},{4,36},{36... | collective-permute-start | bytes 2359304 | tf_op jit(solution)/shard_map/ppermute | solution.py:295
  56.4 1.7 %read_codes.1 = (f32[2,512,512]{2,1,0:T(8,128)S(1)}, f32[2,512,512]{2,1,0:T(8,128)S(1)}) custom-call(s32[2,512,512]{2,1,0:T(8,128)} %labels_hbm.1, bf16[32,72,128]{2,1,0:T(8,128)(2,1)S(1)} %all_to_all.20.gathered_ref.subject_ref, bf16[8,96,512]{2,1,0:T(8,128)(2,1)S(1)} %all_to_all.21.own_ref.refs_0_), custom_call_target="tpu_custom_call" | custom-call | tf_op jit(solution)/shard_map/read_codes/pallas_call | solution.py:284
  58.1 0.5 collective-permute-done.other_ref.refs_1_
  58.7 2.9 %grads.1 = (bf16[8,96,512]{2,1,0:T(8,128)(2,1)S(1)}, bf16[8,96,512]{2,1,0:T(8,128)(2,1)S(1)}, bf16[2,512,512]{2,1,0:T(8,128)(2,1)S(1)}, f32[2,512,512]{2,1,0:T(8,128)S(1)}) custom-call(bf16[32,72,128]{2,1,0:T(8,128)(2,1)S(1)} %all_to_all.20.gathered_ref.subject_ref, bf16[8,96,512]{2,1,0:T(8,128)(2,1)S(1)} %all_to_all.21.own_ref.refs_0_, ...), custom_call_target="tpu_custom_call" | custom-call | tf_op jit(solution)/shard_map/grads/pallas_call | solution.py:284
  61.5 2.0 %collective-permute-start.1 = (bf16[8,96,512]{2,1,0:T(8,128)(2,1)S(1)}, bf16[8,96,512]{2,1,0:T(8,128)(2,1)S(1)}, u32[]{:S(2)}, u32[]{:S(2)}) collective-permute-start(bf16[8,96,512]{2,1,0:T(8,128)(2,1)S(1)} %get-tuple-element.23), channel_id=1, source_target_pairs={{0,32},{32,0},{1,33},{33,1},{2,34},{34,2},{3,35},{35,3},{4,36},{36... | collective-permute-start | bytes 2359304 | tf_op jit(solution)/shard_map/ppermute | solution.py:295
  63.6 1.8 %subject_grads.1 = (bf16[32,64,128]{2,1,0:T(8,128)(2,1)S(1)}, f32[32,128]{1,0:T(8,128)S(1)}) custom-call(bf16[8,96,512]{2,1,0:T(8,128)(2,1)S(1)} %all_to_all.21.own_ref.refs_0_, bf16[8,96,512]{2,1,0:T(8,128)(2,1)S(1)} %collective-permute-done.other_ref.refs_1_, f32[2,512,512]{2,1,0:T(8,128)S(1)} %get-tuple-element.24.refs_2_, ...), custom_call_target="tpu_custom_call" | custom-call | tf_op jit(solution)/shard_map/subject_grads/pallas_call | solution.py:284
  65.4 0.3 collective-permute-done.1.received_ref
  65.7 0.2 add_pair.1
  65.9 15.8 %all_to_all.22.refs_0_.refs_1_ = bf16[8,96,512]{2,1,0:T(8,128)(2,1)S(1)} all-to-all(bf16[8,96,512]{2,1,0:T(8,128)(2,1)S(1)} %add_pair.1), channel_id=1, replica_groups=mesh['chip'=8,'core'=2,'obj'=32] {'chip'}, dimensions={0} | all-to-all | bytes 1572864 | tf_op jit(solution)/shard_map/all_to_all | solution.py:369
  81.7 0.3 sum_relations.1
  82.0 26.6 %all_to_all.23 = bf16[1184,2,128]{2,1,0:T(2,128)(2,1)S(1)} all-to-all(bf16[1184,2,128]{2,1,0:T(2,128)(2,1)S(1)} %bitcast.6), channel_id=1, replica_groups=mesh['chip'=8,'core'=2,'obj'=32] {'obj'}, dimensions={0} | all-to-all | bytes 1212416 | tf_op jit(solution)/shard_map/all_to_all | solution.py:380
  108.6 0.9 sum_factors.1
Async XLA Ops:
  54.5 4.2 %collective-permute-start = (bf16[8,96,512]{2,1,0:T(8,128)(2,1)S(1)}, bf16[8,96,512]{2,1,0:T(8,128)(2,1)S(1)}, u32[]{:S(2)}, u32[]{:S(2)}) collective-permute-start(bf16[8,96,512]{2,1,0:T(8,128)(2,1)S(1)} %all_to_all.21.own_ref.refs_0_), channel_id=1, source_target_pairs={{0,32},{32,0},{1,33},{33,1},{2,34},{34,2},{3,35},{35,3},{4,36},{36... | collective-permute-start | bytes 2359304 | tf_op jit(solution)/shard_map/ppermute | solution.py:295
  61.5 4.2 %collective-permute-start.1 = (bf16[8,96,512]{2,1,0:T(8,128)(2,1)S(1)}, bf16[8,96,512]{2,1,0:T(8,128)(2,1)S(1)}, u32[]{:S(2)}, u32[]{:S(2)}) collective-permute-start(bf16[8,96,512]{2,1,0:T(8,128)(2,1)S(1)} %get-tuple-element.23), channel_id=1, source_target_pairs={{0,32},{32,0},{1,33},{33,1},{2,34},{34,2},{3,35},{35,3},{4,36},{36... | collective-permute-start | bytes 2359304 | tf_op jit(solution)/shard_map/ppermute | solution.py:295

commit v10 on v9

--- a/solution.py
+++ b/solution.py
@@ -95,7 +95,9 @@
         out_ref[p, rows:] = rel
 
 
-def read_codes(labels_hbm, subject_ref, own_ref, sign_ref, half_ref, labels_ref, arrived):
+def read_codes(
+    labels_hbm, subject_ref, own_ref, sign_ref, half_ref, turned_ref, labels_ref, arrived
+):
     relations, size, _ = labels_ref.shape
     loads = [
         pltpu.make_async_copy(labels_hbm.at[k], labels_ref.at[k], arrived.at[k])
@@ -109,6 +111,7 @@
     rows = size // (2 * own_ref.shape[0])
     for k in range(relations):
         half_ref[k] = dot(ours, relation_half(own_ref, k, rows), (1, 0))
+    turned_ref[...] = subject.T
     for k in range(relations):
         loads[k].wait()
         codes = labels_ref[k]
@@ -143,6 +146,7 @@
     other_ref,
     sign_ref,
     half_ref,
+    turned_ref,
     keep_ref,
     send_ref,
     carried_ref,
@@ -175,13 +179,18 @@
         carried_ref[k] = dot(residual_ref[k], objects, (1, 0)).astype(BF16)
 
     def relation_grad(k):
-        grad = dot(subject, carried_ref[k], (0, 0)).astype(BF16).reshape(2, -1, rows, size)
+        grad = dot(turned_ref[...], carried_ref[k], (1, 0)).astype(BF16).reshape(2, -1, rows, size)
         store_owners(keep_ref, send_ref, k + 1, grad[0], grad[1])
 
+    project(0)
+    score(0)
     for k in range(relations):
-        project(k)
-        score(k)
+        more = k + 1 < relations
+        if more:
+            project(k + 1)
         settle(k)
+        if more:
+            score(k + 1)
         if k > 0:
             relation_grad(k - 1)
         carry(k)
@@ -324,10 +333,10 @@
     own = lax.all_to_all(sent, "chip", 0, 0, tiled=True)
     other = to_other_core(own)
     square = (count, subjects, width)
-    sign, half = call(
+    sign, half, transposed = call(
         read_codes,
         "read_codes",
-        (shape(labels.shape, F32), shape(square, F32)),
+        (shape(labels.shape, F32), shape(square, F32), shape((width, subjects))),
         labels,
         subject_all,
         own,
@@ -343,6 +352,7 @@
         other,
         sign,
         half,
+        transposed,
         scratch=[pltpu.VMEM(square, BF16), pltpu.VMEM(labels.shape, BF16)],
     )
     swapped = to_other_core(send)

time: 110 us -> 110 us (level)
  no operation moved by 1% of the time
where the time goes in v10:
time: 110 us
  blocking collectives  95.2 us (87%)
  Pallas kernels  8.83 us (8%)
  starting transfers between devices  3.94 us (4%)
    all_to_all x1, blocking collectives, body(): subject_all = lax.all_to_all(sent, 'obj', 0, 0, tiled=True)  37.5 us
    all_to_all x1, blocking collectives, body(): received = lax.all_to_all(sent, 'obj', 0, 0, tiled=True).reshape(-1, LANES)  26.6 us
    all_to_all x1, blocking collectives, body(): object_partial = lax.all_to_all(sent, 'chip', 0, 0, tiled=True)  15.8 us
    all_to_all x1, blocking collectives, body(): own = lax.all_to_all(sent, 'chip', 0, 0, tiled=True)  15.3 us
    pallas_call x8, Pallas kernels, call(): pl.pallas_call(kernel, out_shape=outs, in_specs=[pl.BlockSpec(memory_spac...  8.83 us
    ppermute x2, starting transfers between devices, to_other_core(): return lax.ppermute(array, 'core', [(0, 1), (1, 0)])  3.94 us
  transfers between devices with their start and end apart: 2, of which 2 were waited for; matrix products, arithmetic and copies ran while one was open for 0% of the time, Pallas kernels for 3%

profile of v10, /device:TPU:8, one launch (start us, length us, event | category | flops | bytes accessed | tf_op | source)
XLA Modules:
  0.0 109.6 jit_solution(5979254697596371762)
XLA Ops:
  0.6 0.9 pack_subject.1
  1.5 37.5 %all_to_all.20.gathered_ref.subject_ref = bf16[32,72,128]{2,1,0:T(8,128)(2,1)S(1)} all-to-all(bf16[32,72,128]{2,1,0:T(8,128)(2,1)S(1)} %get-tuple-element.19), channel_id=1, replica_groups=mesh['chip'=8,'core'=2,'obj'=32] {'obj'}, dimensions={0} | all-to-all | bytes 1179648 | tf_op jit(solution)/shard_map/all_to_all | solution.py:330
  39.0 0.2 pack_object.1
  39.2 15.3 %all_to_all.21.own_ref.refs_0_ = bf16[8,96,512]{2,1,0:T(8,128)(2,1)S(1)} all-to-all(bf16[8,96,512]{2,1,0:T(8,128)(2,1)S(1)} %pack_object.1), channel_id=1, replica_groups=mesh['chip'=8,'core'=2,'obj'=32] {'chip'}, dimensions={0} | all-to-all | bytes 1572864 | tf_op jit(solution)/shard_map/all_to_all | solution.py:333
  54.5 1.9 %collective-permute-start = (bf16[8,96,512]{2,1,0:T(8,128)(2,1)S(1)}, bf16[8,96,512]{2,1,0:T(8,128)(2,1)S(1)}, u32[]{:S(2)}, u32[]{:S(2)}) collective-permute-start(bf16[8,96,512]{2,1,0:T(8,128)(2,1)S(1)} %all_to_all.21.own_ref.refs_0_), channel_id=1, source_target_pairs={{0,32},{32,0},{1,33},{33,1},{2,34},{34,2},{3,35},{35,3},{4,36},{36... | collective-permute-start | bytes 2359304 | tf_op jit(solution)/shard_map/ppermute | solution.py:304
  56.4 1.7 %read_codes.1 = (f32[2,512,512]{2,1,0:T(8,128)S(1)}, f32[2,512,512]{2,1,0:T(8,128)S(1)}, bf16[512,512]{1,0:T(8,128)(2,1)S(1)}) custom-call(s32[2,512,512]{2,1,0:T(8,128)} %labels_hbm.1, bf16[32,72,128]{2,1,0:T(8,128)(2,1)S(1)} %all_to_all.20.gathered_ref.subject_ref, bf16[8,96,512]{2,1,0:T(8,128)(2,1)S(1)} %all_to_all.21.own_ref.refs_0_), custom_call_target="tpu_custom_call" | custom-call | tf_op jit(solution)/shard_map/read_codes/pallas_call | solution.py:293
  58.1 0.5 collective-permute-done.other_ref.refs_1_
  58.7 2.9 %grads.1 = (bf16[8,96,512]{2,1,0:T(8,128)(2,1)S(1)}, bf16[8,96,512]{2,1,0:T(8,128)(2,1)S(1)}, bf16[2,512,512]{2,1,0:T(8,128)(2,1)S(1)}, f32[2,512,512]{2,1,0:T(8,128)S(1)}) custom-call(bf16[32,72,128]{2,1,0:T(8,128)(2,1)S(1)} %all_to_all.20.gathered_ref.subject_ref, bf16[8,96,512]{2,1,0:T(8,128)(2,1)S(1)} %all_to_all.21.own_ref.refs_0_, ...), custom_call_target="tpu_custom_call" | custom-call | tf_op jit(solution)/shard_map/grads/pallas_call | solution.py:293
  61.6 2.0 %collective-permute-start.1 = (bf16[8,96,512]{2,1,0:T(8,128)(2,1)S(1)}, bf16[8,96,512]{2,1,0:T(8,128)(2,1)S(1)}, u32[]{:S(2)}, u32[]{:S(2)}) collective-permute-start(bf16[8,96,512]{2,1,0:T(8,128)(2,1)S(1)} %get-tuple-element.25), channel_id=1, source_target_pairs={{0,32},{32,0},{1,33},{33,1},{2,34},{34,2},{3,35},{35,3},{4,36},{36... | collective-permute-start | bytes 2359304 | tf_op jit(solution)/shard_map/ppermute | solution.py:304
  63.6 1.8 %subject_grads.1 = (bf16[32,64,128]{2,1,0:T(8,128)(2,1)S(1)}, f32[32,128]{1,0:T(8,128)S(1)}) custom-call(bf16[8,96,512]{2,1,0:T(8,128)(2,1)S(1)} %all_to_all.21.own_ref.refs_0_, bf16[8,96,512]{2,1,0:T(8,128)(2,1)S(1)} %collective-permute-done.other_ref.refs_1_, f32[2,512,512]{2,1,0:T(8,128)S(1)} %get-tuple-element.26.refs_2_, ...), custom_call_target="tpu_custom_call" | custom-call | tf_op jit(solution)/shard_map/subject_grads/pallas_call | solution.py:293
  65.4 0.4 collective-permute-done.1.received_ref
  65.8 0.2 add_pair.1
  66.0 15.8 %all_to_all.22.refs_0_.refs_1_ = bf16[8,96,512]{2,1,0:T(8,128)(2,1)S(1)} all-to-all(bf16[8,96,512]{2,1,0:T(8,128)(2,1)S(1)} %add_pair.1), channel_id=1, replica_groups=mesh['chip'=8,'core'=2,'obj'=32] {'chip'}, dimensions={0} | all-to-all | bytes 1572864 | tf_op jit(solution)/shard_map/all_to_all | solution.py:379
  81.8 0.3 sum_relations.1
  82.1 26.6 %all_to_all.23 = bf16[1184,2,128]{2,1,0:T(2,128)(2,1)S(1)} all-to-all(bf16[1184,2,128]{2,1,0:T(2,128)(2,1)S(1)} %bitcast.6), channel_id=1, replica_groups=mesh['chip'=8,'core'=2,'obj'=32] {'obj'}, dimensions={0} | all-to-all | bytes 1212416 | tf_op jit(solution)/shard_map/all_to_all | solution.py:390
  108.7 0.9 sum_factors.1
Async XLA Ops:
  54.5 4.2 %collective-permute-start = (bf16[8,96,512]{2,1,0:T(8,128)(2,1)S(1)}, bf16[8,96,512]{2,1,0:T(8,128)(2,1)S(1)}, u32[]{:S(2)}, u32[]{:S(2)}) collective-permute-start(bf16[8,96,512]{2,1,0:T(8,128)(2,1)S(1)} %all_to_all.21.own_ref.refs_0_), channel_id=1, source_target_pairs={{0,32},{32,0},{1,33},{33,1},{2,34},{34,2},{3,35},{35,3},{4,36},{36... | collective-permute-start | bytes 2359304 | tf_op jit(solution)/shard_map/ppermute | solution.py:304
  61.6 4.2 %collective-permute-start.1 = (bf16[8,96,512]{2,1,0:T(8,128)(2,1)S(1)}, bf16[8,96,512]{2,1,0:T(8,128)(2,1)S(1)}, u32[]{:S(2)}, u32[]{:S(2)}) collective-permute-start(bf16[8,96,512]{2,1,0:T(8,128)(2,1)S(1)} %get-tuple-element.25), channel_id=1, source_target_pairs={{0,32},{32,0},{1,33},{33,1},{2,34},{34,2},{3,35},{35,3},{4,36},{36... | collective-permute-start | bytes 2359304 | tf_op jit(solution)/shard_map/ppermute | solution.py:304

commit v11 on v10

--- a/solution.py
+++ b/solution.py
@@ -203,7 +203,7 @@
 
 
 def add_pair(keep_ref, received_ref, _, out_ref):
-    out_ref[...] = (keep_ref[...].astype(F32) + received_ref[...].astype(F32)).astype(BF16)
+    out_ref[...] = keep_ref[...] + received_ref[...]
 
 
 def subject_grads(

time: 110 us -> 110 us (level)
  no operation moved by 1% of the time
where the time goes in v11:
time: 110 us; the launch traced here: 109 us
  blocking collectives  95.2 us (87%)
  Pallas kernels  8.73 us (8%)
  starting transfers between devices  3.94 us (4%)
    all_to_all x1, blocking collectives, body(): subject_all = lax.all_to_all(sent, 'obj', 0, 0, tiled=True)  37.5 us
    all_to_all x1, blocking collectives, body(): received = lax.all_to_all(sent, 'obj', 0, 0, tiled=True).reshape(-1, LANES)  26.6 us
    all_to_all x1, blocking collectives, body(): object_partial = lax.all_to_all(sent, 'chip', 0, 0, tiled=True)  15.8 us
    all_to_all x1, blocking collectives, body(): own = lax.all_to_all(sent, 'chip', 0, 0, tiled=True)  15.3 us
    pallas_call x8, Pallas kernels, call(): pl.pallas_call(kernel, out_shape=outs, in_specs=[pl.BlockSpec(memory_spac...  8.73 us
    ppermute x2, starting transfers between devices, to_other_core(): return lax.ppermute(array, 'core', [(0, 1), (1, 0)])  3.94 us
  transfers between devices with their start and end apart: 2, of which 2 were waited for; matrix products, arithmetic and copies ran while one was open for 0% of the time, Pallas kernels for 3%

profile of v11, /device:TPU:8, one launch (start us, length us, event | category | flops | bytes accessed | tf_op | source)
XLA Modules:
  0.0 109.5 jit_solution(17479753882682362838)
XLA Ops:
  0.6 0.9 pack_subject.1
  1.5 37.5 %all_to_all.20.gathered_ref.subject_ref = bf16[32,72,128]{2,1,0:T(8,128)(2,1)S(1)} all-to-all(bf16[32,72,128]{2,1,0:T(8,128)(2,1)S(1)} %get-tuple-element.19), channel_id=1, replica_groups=mesh['chip'=8,'core'=2,'obj'=32] {'obj'}, dimensions={0} | all-to-all | bytes 1179648 | tf_op jit(solution)/shard_map/all_to_all | solution.py:330
  39.0 0.2 pack_object.1
  39.2 15.3 %all_to_all.21.own_ref.refs_0_ = bf16[8,96,512]{2,1,0:T(8,128)(2,1)S(1)} all-to-all(bf16[8,96,512]{2,1,0:T(8,128)(2,1)S(1)} %pack_object.1), channel_id=1, replica_groups=mesh['chip'=8,'core'=2,'obj'=32] {'chip'}, dimensions={0} | all-to-all | bytes 1572864 | tf_op jit(solution)/shard_map/all_to_all | solution.py:333
  54.5 1.9 %collective-permute-start = (bf16[8,96,512]{2,1,0:T(8,128)(2,1)S(1)}, bf16[8,96,512]{2,1,0:T(8,128)(2,1)S(1)}, u32[]{:S(2)}, u32[]{:S(2)}) collective-permute-start(bf16[8,96,512]{2,1,0:T(8,128)(2,1)S(1)} %all_to_all.21.own_ref.refs_0_), channel_id=1, source_target_pairs={{0,32},{32,0},{1,33},{33,1},{2,34},{34,2},{3,35},{35,3},{4,36},{36... | collective-permute-start | bytes 2359304 | tf_op jit(solution)/shard_map/ppermute | solution.py:304
  56.4 1.7 %read_codes.1 = (f32[2,512,512]{2,1,0:T(8,128)S(1)}, f32[2,512,512]{2,1,0:T(8,128)S(1)}, bf16[512,512]{1,0:T(8,128)(2,1)S(1)}) custom-call(s32[2,512,512]{2,1,0:T(8,128)} %labels_hbm.1, bf16[32,72,128]{2,1,0:T(8,128)(2,1)S(1)} %all_to_all.20.gathered_ref.subject_ref, bf16[8,96,512]{2,1,0:T(8,128)(2,1)S(1)} %all_to_all.21.own_ref.refs_0_), custom_call_target="tpu_custom_call" | custom-call | tf_op jit(solution)/shard_map/read_codes/pallas_call | solution.py:293
  58.1 0.5 collective-permute-done.other_ref.refs_1_
  58.7 2.9 %grads.1 = (bf16[8,96,512]{2,1,0:T(8,128)(2,1)S(1)}, bf16[8,96,512]{2,1,0:T(8,128)(2,1)S(1)}, bf16[2,512,512]{2,1,0:T(8,128)(2,1)S(1)}, f32[2,512,512]{2,1,0:T(8,128)S(1)}) custom-call(bf16[32,72,128]{2,1,0:T(8,128)(2,1)S(1)} %all_to_all.20.gathered_ref.subject_ref, bf16[8,96,512]{2,1,0:T(8,128)(2,1)S(1)} %all_to_all.21.own_ref.refs_0_, ...), custom_call_target="tpu_custom_call" | custom-call | tf_op jit(solution)/shard_map/grads/pallas_call | solution.py:293
  61.6 2.0 %collective-permute-start.1 = (bf16[8,96,512]{2,1,0:T(8,128)(2,1)S(1)}, bf16[8,96,512]{2,1,0:T(8,128)(2,1)S(1)}, u32[]{:S(2)}, u32[]{:S(2)}) collective-permute-start(bf16[8,96,512]{2,1,0:T(8,128)(2,1)S(1)} %get-tuple-element.25), channel_id=1, source_target_pairs={{0,32},{32,0},{1,33},{33,1},{2,34},{34,2},{3,35},{35,3},{4,36},{36... | collective-permute-start | bytes 2359304 | tf_op jit(solution)/shard_map/ppermute | solution.py:304
  63.6 1.8 %subject_grads.1 = (bf16[32,64,128]{2,1,0:T(8,128)(2,1)S(1)}, f32[32,128]{1,0:T(8,128)S(1)}) custom-call(bf16[8,96,512]{2,1,0:T(8,128)(2,1)S(1)} %all_to_all.21.own_ref.refs_0_, bf16[8,96,512]{2,1,0:T(8,128)(2,1)S(1)} %collective-permute-done.other_ref.refs_1_, f32[2,512,512]{2,1,0:T(8,128)S(1)} %get-tuple-element.26.refs_2_, ...), custom_call_target="tpu_custom_call" | custom-call | tf_op jit(solution)/shard_map/subject_grads/pallas_call | solution.py:293
  65.4 0.4 collective-permute-done.1.received_ref
  65.8 0.1 add_pair.1
  65.9 15.8 %all_to_all.22.refs_0_.refs_1_ = bf16[8,96,512]{2,1,0:T(8,128)(2,1)S(1)} all-to-all(bf16[8,96,512]{2,1,0:T(8,128)(2,1)S(1)} %add_pair.1), channel_id=1, replica_groups=mesh['chip'=8,'core'=2,'obj'=32] {'chip'}, dimensions={0} | all-to-all | bytes 1572864 | tf_op jit(solution)/shard_map/all_to_all | solution.py:379
  81.7 0.3 sum_relations.1
  82.0 26.6 %all_to_all.23 = bf16[1184,2,128]{2,1,0:T(2,128)(2,1)S(1)} all-to-all(bf16[1184,2,128]{2,1,0:T(2,128)(2,1)S(1)} %bitcast.6), channel_id=1, replica_groups=mesh['chip'=8,'core'=2,'obj'=32] {'obj'}, dimensions={0} | all-to-all | bytes 1212416 | tf_op jit(solution)/shard_map/all_to_all | solution.py:390
  108.6 0.9 sum_factors.1
Async XLA Ops:
  54.5 4.2 %collective-permute-start = (bf16[8,96,512]{2,1,0:T(8,128)(2,1)S(1)}, bf16[8,96,512]{2,1,0:T(8,128)(2,1)S(1)}, u32[]{:S(2)}, u32[]{:S(2)}) collective-permute-start(bf16[8,96,512]{2,1,0:T(8,128)(2,1)S(1)} %all_to_all.21.own_ref.refs_0_), channel_id=1, source_target_pairs={{0,32},{32,0},{1,33},{33,1},{2,34},{34,2},{3,35},{35,3},{4,36},{36... | collective-permute-start | bytes 2359304 | tf_op jit(solution)/shard_map/ppermute | solution.py:304
  61.6 4.2 %collective-permute-start.1 = (bf16[8,96,512]{2,1,0:T(8,128)(2,1)S(1)}, bf16[8,96,512]{2,1,0:T(8,128)(2,1)S(1)}, u32[]{:S(2)}, u32[]{:S(2)}) collective-permute-start(bf16[8,96,512]{2,1,0:T(8,128)(2,1)S(1)} %get-tuple-element.25), channel_id=1, source_target_pairs={{0,32},{32,0},{1,33},{33,1},{2,34},{34,2},{3,35},{35,3},{4,36},{36... | collective-permute-start | bytes 2359304 | tf_op jit(solution)/shard_map/ppermute | solution.py:304
